TPU v7x, 32 devices: a whole 2x2x4 slice. The times are simulated.
32 devices in a mesh: dp: 4 (over z), fsdp: 8 (over y, x, core).
Axes of the slice: x: 2, y: 2, z: 4, core: 2. Of those that a mesh axis runs over, the one named last changes fastest.
Arguments:
- layer_input: bfloat16 [2, 6144, 2048], P(None, ('dp', 'fsdp')), may hold values from -6 to 6
- segment_ids: int32 [2, 6144], P(None, ('dp', 'fsdp')), may hold values from 0 to 383, as said below
- live_counts: int32 [2, 32], P(None, ('dp', 'fsdp')), may hold values from 96 to 192, as said below
- w_query: bfloat16 [2048, 2048], P(('dp', 'fsdp')), may hold values from -0.125 to 0.125
- w_key: bfloat16 [2048, 256], P(('dp', 'fsdp')), may hold values from -0.125 to 0.125
- w_value: bfloat16 [2048, 256], P(('dp', 'fsdp')), may hold values from -0.125 to 0.125
- w_out: bfloat16 [2048, 2048], P(('dp', 'fsdp')), may hold values from -0.375 to 0.375
- w_gate: bfloat16 [2048, 5632], P(('dp', 'fsdp')), may hold values from -0.125 to 0.125
- w_up: bfloat16 [2048, 5632], P(('dp', 'fsdp')), may hold values from -0.125 to 0.125
- w_down: bfloat16 [5632, 2048], P(('dp', 'fsdp')), may hold values from -0.078125 to 0.078125
- attn_gain: bfloat16 [2048], P(('dp', 'fsdp')), may hold values from 0.5 to 1.5
- mlp_gain: bfloat16 [2048], P(('dp', 'fsdp')), may hold values from 0.5 to 1.5
- out_grad: bfloat16 [2, 6144, 2048], P(None, ('dp', 'fsdp')), may hold values from -6 to 6
Outputs:
- layer_output: bfloat16 [2, 6144, 2048], P(None, ('dp', 'fsdp'))
- input_grad: float32 [2, 6144, 2048], P(None, ('dp', 'fsdp'))
- grad_w_query: float32 [2048, 2048], P(('dp', 'fsdp'))
- grad_w_key: float32 [2048, 256], P(('dp', 'fsdp'))
- grad_w_value: float32 [2048, 256], P(('dp', 'fsdp'))
- grad_w_out: float32 [2048, 2048], P(('dp', 'fsdp'))
- grad_w_gate: float32 [2048, 5632], P(('dp', 'fsdp'))
- grad_w_up: float32 [2048, 5632], P(('dp', 'fsdp'))
- grad_w_down: float32 [5632, 2048], P(('dp', 'fsdp'))
- grad_attn_gain: float32 [2048], P(('dp', 'fsdp'))
- grad_mlp_gain: float32 [2048], P(('dp', 'fsdp'))
Inputs may be any that keep to these rules, and one draw needn't show every extreme that they name: `segment_ids`: within each device's block segment numbers never fall; live slots come first, with segment numbers from 0, and padding slot at place i of the block has the number 192 + i. Some block is one whole sequence of 192 live tokens. `live_counts`: live tokens of each device's block.
All inputs are finite; a program needn't handle non-finite values.
Results may differ from a plain program's by a relative error of at most 0.013.
Values may be sent and summed in bfloat16 or wider, within the bound.
No kernel may reach another device: no remote copies, remote signals or barrier semaphores. Data moves between devices by JAX's collectives and lax.ppermute only.
A program may use at most 384 MiB of HBM per device.

v0:
```python
import jax
import jax.numpy as jnp
from jax import lax
from jax.sharding import PartitionSpec as P

HEADS = 32
KV_HEADS = 4
HEAD_DIM = 64
MICRO = 2


EPS = 1e-05


def inner_rows(left, right):
    return lax.dot_general(
        left, right, (((0,), (0,)), ((), ())), preferred_element_type=jnp.float32
    )


def against(left, weight):
    return lax.dot_general(
        left, weight, (((1,), (1,)), ((), ())), preferred_element_type=jnp.float32
    )


def forward_dot(left, weight):
    return jnp.dot(left, weight, preferred_element_type=jnp.float32)


def positions(segment):
    place = jnp.arange(segment.shape[0], dtype=jnp.int32)
    before = jnp.concatenate([segment[:1] - 1, segment[:-1]])
    start = lax.cummax(jnp.where(segment != before, place, 0), axis=0)
    return place - start


def rope_tables(pos):
    steps = jnp.arange(HEAD_DIM // 2, dtype=jnp.int32).astype(jnp.float32)
    freq = 10000.0 ** (-2.0 * steps / HEAD_DIM)
    angle = pos.astype(jnp.float32)[:, None] * freq[None, :]
    cos_half = jnp.cos(angle)
    sin_half = jnp.sin(angle)
    return (
        jnp.concatenate([cos_half, cos_half], axis=-1),
        jnp.concatenate([sin_half, sin_half], axis=-1),
    )


def rotate(value, cos_t, sin_t):
    half = HEAD_DIM // 2
    turned = jnp.concatenate([-value[..., half:], value[..., :half]], axis=-1)
    return value * cos_t[:, None, :] + turned * sin_t[:, None, :]


def norm_back(normed, scale_r, grad_normed):
    return scale_r * (grad_normed - normed * jnp.mean(grad_normed * normed, axis=-1, keepdims=True))


def local(
    layer_input,
    segment_ids,
    live_counts,
    w_query,
    w_key,
    w_value,
    w_out,
    w_gate,
    w_up,
    w_down,
    attn_gain,
    mlp_gain,
    out_grad,
):
    rows = layer_input.shape[1]
    group = HEADS // KV_HEADS
    width = HEADS * HEAD_DIM
    scaling = HEAD_DIM ** (-0.5)
    span = jnp.arange(rows, dtype=jnp.int32)
    outputs = []
    input_grads = []
    attn_total = None
    mlp_total = None
    kept_mlp = []
    kept_attn = []
    gain_two_sum = None
    gain_one_sum = None
    for micro in range(MICRO):
        segment = segment_ids[micro]
        valid = (span < live_counts[micro, 0]).astype(jnp.float32)[:, None]
        cos_t, sin_t = rope_tables(positions(segment))
        allow = (segment[:, None] == segment[None, :]) & (span[None, :] <= span[:, None])
        wq_a, wk_a, wv_a, wo_a, g1_a = (
            lax.all_gather(w_query, ("dp", "fsdp"), axis=0, tiled=True),
            lax.all_gather(w_key, ("dp", "fsdp"), axis=0, tiled=True),
            lax.all_gather(w_value, ("dp", "fsdp"), axis=0, tiled=True),
            lax.all_gather(w_out, ("dp", "fsdp"), axis=0, tiled=True),
            lax.all_gather(attn_gain, ("dp", "fsdp"), axis=0, tiled=True),
        )
        inputs = layer_input[micro].astype(jnp.float32)
        r1 = lax.rsqrt(jnp.mean(inputs * inputs, axis=-1, keepdims=True) + EPS)
        n1 = inputs * r1
        gain1 = g1_a.astype(jnp.float32)
        h1 = (n1 * gain1).astype(jnp.bfloat16)
        query = forward_dot(h1, wq_a).reshape(rows, HEADS, HEAD_DIM)
        keys = forward_dot(h1, wk_a).reshape(rows, KV_HEADS, HEAD_DIM)
        values = forward_dot(h1, wv_a).astype(jnp.bfloat16).reshape(rows, KV_HEADS, HEAD_DIM)
        q_rot = (
            rotate(query, cos_t, sin_t)
            .astype(jnp.bfloat16)
            .reshape(rows, KV_HEADS, group, HEAD_DIM)
        )
        k_rot = rotate(keys, cos_t, sin_t).astype(jnp.bfloat16)
        scores = (
            jnp.einsum("qkgd,skd->kgqs", q_rot, k_rot, preferred_element_type=jnp.float32) * scaling
        )
        probs = jax.nn.softmax(jnp.where(allow, scores, -1000000000.0), axis=-1)
        probs_b = probs.astype(jnp.bfloat16)
        mixed = jnp.einsum("kgqs,skd->qkgd", probs_b, values, preferred_element_type=jnp.float32)
        mixed = mixed.reshape(rows, width).astype(jnp.bfloat16)
        hidden = inputs + forward_dot(mixed, wo_a)
        wg_a, wu_a, wd_a, g2_a = (
            lax.all_gather(w_gate, ("dp", "fsdp"), axis=0, tiled=True),
            lax.all_gather(w_up, ("dp", "fsdp"), axis=0, tiled=True),
            lax.all_gather(w_down, ("dp", "fsdp"), axis=0, tiled=True),
            lax.all_gather(mlp_gain, ("dp", "fsdp"), axis=0, tiled=True),
        )
        r2 = lax.rsqrt(jnp.mean(hidden * hidden, axis=-1, keepdims=True) + EPS)
        n2 = hidden * r2
        gain2 = g2_a.astype(jnp.float32)
        h2 = (n2 * gain2).astype(jnp.bfloat16)
        gate = forward_dot(h2, wg_a)
        upward = forward_dot(h2, wu_a)
        sigma = jax.nn.sigmoid(gate)
        silu_gate = gate * sigma
        inner = (silu_gate * upward).astype(jnp.bfloat16)
        result = hidden + forward_dot(inner, wd_a)
        outputs.append((result * valid).astype(jnp.bfloat16))
        wg_b, wu_b, wd_b, g2_b = (
            lax.all_gather(w_gate, ("dp", "fsdp"), axis=0, tiled=True),
            lax.all_gather(w_up, ("dp", "fsdp"), axis=0, tiled=True),
            lax.all_gather(w_down, ("dp", "fsdp"), axis=0, tiled=True),
            lax.all_gather(mlp_gain, ("dp", "fsdp"), axis=0, tiled=True),
        )
        error_rows = out_grad[micro].astype(jnp.float32) * valid
        error_low = error_rows.astype(jnp.bfloat16)
        grad_inner = against(error_low, wd_b)
        grad_gate = (grad_inner * upward * (sigma + gate * sigma * (1.0 - sigma))).astype(
            jnp.bfloat16
        )
        grad_up = (grad_inner * silu_gate).astype(jnp.bfloat16)
        grad_h2 = against(grad_gate, wg_b) + against(grad_up, wu_b)
        grad_g2 = jnp.sum(n2 * grad_h2, axis=0)
        grad_hidden = error_rows + norm_back(n2, r2, grad_h2 * g2_b.astype(jnp.float32))
        kept_mlp.append((h2, grad_gate, grad_up, inner, error_low))
        gain_two_sum = grad_g2 if gain_two_sum is None else gain_two_sum + grad_g2
        wq_b, wk_b, wv_b, wo_b, g1_b = (
            lax.all_gather(w_query, ("dp", "fsdp"), axis=0, tiled=True),
            lax.all_gather(w_key, ("dp", "fsdp"), axis=0, tiled=True),
            lax.all_gather(w_value, ("dp", "fsdp"), axis=0, tiled=True),
            lax.all_gather(w_out, ("dp", "fsdp"), axis=0, tiled=True),
            lax.all_gather(attn_gain, ("dp", "fsdp"), axis=0, tiled=True),
        )
        grad_hidden_b = grad_hidden.astype(jnp.bfloat16)
        grad_mixed = (
            against(grad_hidden_b, wo_b)
            .astype(jnp.bfloat16)
            .reshape(rows, KV_HEADS, group, HEAD_DIM)
        )
        grad_probs = jnp.einsum(
            "qkgd,skd->kgqs", grad_mixed, values, preferred_element_type=jnp.float32
        )
        grad_scores = probs * (grad_probs - jnp.sum(grad_probs * probs, axis=-1, keepdims=True))
        grad_scores = grad_scores.astype(jnp.bfloat16)
        grad_values = jnp.einsum(
            "kgqs,qkgd->skd", probs_b, grad_mixed, preferred_element_type=jnp.float32
        )
        grad_values = grad_values.astype(jnp.bfloat16).reshape(rows, KV_HEADS * HEAD_DIM)
        grad_qrot = (
            jnp.einsum("kgqs,skd->qkgd", grad_scores, k_rot, preferred_element_type=jnp.float32)
            * scaling
        )
        grad_krot = (
            jnp.einsum("kgqs,qkgd->skd", grad_scores, q_rot, preferred_element_type=jnp.float32)
            * scaling
        )
        grad_query = rotate(grad_qrot.reshape(rows, HEADS, HEAD_DIM), cos_t, -sin_t)
        grad_query = grad_query.astype(jnp.bfloat16).reshape(rows, width)
        grad_keys = (
            rotate(grad_krot, cos_t, -sin_t).astype(jnp.bfloat16).reshape(rows, KV_HEADS * HEAD_DIM)
        )
        grad_h1 = against(grad_query, wq_b) + against(grad_keys, wk_b) + against(grad_values, wv_b)
        grad_g1 = jnp.sum(n1 * grad_h1, axis=0)
        input_grads.append(grad_hidden + norm_back(n1, r1, grad_h1 * g1_b.astype(jnp.float32)))
        kept_attn.append((h1, grad_query, grad_keys, grad_values, mixed, grad_hidden_b))
        gain_one_sum = grad_g1 if gain_one_sum is None else gain_one_sum + grad_g1
    stacked = [jnp.concatenate([item[index] for item in kept_mlp], axis=0) for index in range(5)]
    grad_wg = inner_rows(stacked[0], stacked[1])
    grad_wu = inner_rows(stacked[0], stacked[2])
    grad_wd = inner_rows(stacked[3], stacked[4])
    mlp_total = (
        lax.psum_scatter(grad_wg, ("dp", "fsdp"), scatter_dimension=0, tiled=True),
        lax.psum_scatter(grad_wu, ("dp", "fsdp"), scatter_dimension=0, tiled=True),
        lax.psum_scatter(grad_wd, ("dp", "fsdp"), scatter_dimension=0, tiled=True),
        lax.psum_scatter(gain_two_sum, ("dp", "fsdp"), scatter_dimension=0, tiled=True),
    )
    joined = [jnp.concatenate([item[index] for item in kept_attn], axis=0) for index in range(6)]
    grad_wq = inner_rows(joined[0], joined[1])
    grad_wk = inner_rows(joined[0], joined[2])
    grad_wv = inner_rows(joined[0], joined[3])
    grad_wo = inner_rows(joined[4], joined[5])
    attn_total = (
        lax.psum_scatter(grad_wq, ("dp", "fsdp"), scatter_dimension=0, tiled=True),
        lax.psum_scatter(grad_wk, ("dp", "fsdp"), scatter_dimension=0, tiled=True),
        lax.psum_scatter(grad_wv, ("dp", "fsdp"), scatter_dimension=0, tiled=True),
        lax.psum_scatter(grad_wo, ("dp", "fsdp"), scatter_dimension=0, tiled=True),
        lax.psum_scatter(gain_one_sum, ("dp", "fsdp"), scatter_dimension=0, tiled=True),
    )
    layer_output = jnp.stack(outputs, axis=0)
    input_grad = jnp.stack(input_grads, axis=0)
    return (
        layer_output,
        input_grad,
        attn_total[0],
        attn_total[1],
        attn_total[2],
        attn_total[3],
        mlp_total[0],
        mlp_total[1],
        mlp_total[2],
        attn_total[4],
        mlp_total[3],
    )


def solution(mesh):
    in_specs = (
        P(None, ("dp", "fsdp"), None),
        P(None, ("dp", "fsdp")),
        P(None, ("dp", "fsdp")),
        P(("dp", "fsdp"), None),
        P(("dp", "fsdp"), None),
        P(("dp", "fsdp"), None),
        P(("dp", "fsdp"), None),
        P(("dp", "fsdp"), None),
        P(("dp", "fsdp"), None),
        P(("dp", "fsdp"), None),
        P(("dp", "fsdp")),
        P(("dp", "fsdp")),
        P(None, ("dp", "fsdp"), None),
    )
    out_specs = (
        P(None, ("dp", "fsdp"), None),
        P(None, ("dp", "fsdp"), None),
        P(("dp", "fsdp"), None),
        P(("dp", "fsdp"), None),
        P(("dp", "fsdp"), None),
        P(("dp", "fsdp"), None),
        P(("dp", "fsdp"), None),
        P(("dp", "fsdp"), None),
        P(("dp", "fsdp"), None),
        P(("dp", "fsdp")),
        P(("dp", "fsdp")),
    )
    return jax.shard_map(local, mesh=mesh, in_specs=in_specs, out_specs=out_specs, check_vma=False)
```

profile of v0, /device:TPU:0, one launch (start us, length us, event | category | flops | bytes accessed | tf_op | source)
XLA Modules:
  0.0 3000.6 jit_solution(7381076084730386270)
XLA Ops:
  15.4 42.2 %all-reduce.7 = (bf16[2048]{0:T(1024)(128)(2,1)S(1)}, bf16[2048]{0:T(1024)(128)(2,1)S(1)}) all-reduce(bf16[2048]{0:T(1024)(128)(2,1)S(1)} %dynamic-update-slice, bf16[2048]{0:T(1024)(128)(2,1)S(1)} %dynamic-update-slice.1), channel_id=1, replica_groups=mesh['dp'=4,'fsdp'=8] {'dp','fsdp'}, use_global_device_ids=true, to_apply=%add.2 | all-reduce | flops 4096 | bytes 16384
  63.4 1.5 fusion.93
  65.4 2.0 all-gather.10.cloned.1.call-done
  67.4 2.3 copy.57
  69.6 53.3 %all-gather.8.cloned.1.call-done = bf16[2048,256]{1,0:T(8,128)(2,1)} async-done(((bf16[64,256]{1,0:T(8,128)(2,1)}), bf16[2048,256]{1,0:T(8,128)(2,1)}) %all-gather.8.cloned.1.call-update) | async-done | bytes 1048592 | tf_op jit(solution)/shard_map/all_gather | solution.py:96
  123.0 1.6 convolution_convert_fusion.3
  125.3 1.6 convolution_convert_fusion.2
  127.7 1.8 fusion.148
  130.2 71.7 %all-gather.12.cloned.1.call-done = bf16[2048,2048]{1,0:T(8,128)(2,1)} async-done(((bf16[64,2048]{1,0:T(8,128)(2,1)}), bf16[2048,2048]{1,0:T(8,128)(2,1)}) %all-gather.12.cloned.1.call-update) | async-done | bytes 8388624 | tf_op jit(solution)/shard_map/all_gather | solution.py:94
  201.9 12.4 copy.58
  214.3 5.8 fusion.146
  221.2 5.0 fusion.176
  226.1 4.5 fusion.102
  230.6 49.7 %all-gather.14.cloned.1.call-done = bf16[2048,2048]{1,0:T(8,128)(2,1)} async-done(((bf16[64,2048]{1,0:T(8,128)(2,1)}), bf16[2048,2048]{1,0:T(8,128)(2,1)}) %all-gather.14.cloned.1.call-update) | async-done | bytes 8388624 | tf_op jit(solution)/shard_map/all_gather | solution.py:97
  280.3 5.6 multiply_reduce_fusion.5
  286.0 6.6 fusion.150
  292.8 1.4 fusion.39
  294.3 6.4 fusion.175
  300.6 3.5 fusion.105
  304.2 6.8 multiply_reduce_fusion.4
  311.2 114.4 %all-gather.16.cloned.1.call-done = bf16[2048,5632]{1,0:T(8,128)(2,1)} async-done(((bf16[64,5632]{1,0:T(8,128)(2,1)}), bf16[2048,5632]{1,0:T(8,128)(2,1)}) %all-gather.16.cloned.1.call-update) | async-done | bytes 23068688 | tf_op jit(solution)/shard_map/all_gather | solution.py:123
  425.5 12.1 fusion.177
  437.6 132.7 %all-gather.18.cloned.1.call-done = bf16[2048,5632]{1,0:T(8,128)(2,1)} async-done(((bf16[64,5632]{1,0:T(8,128)(2,1)}), bf16[2048,5632]{1,0:T(8,128)(2,1)}) %all-gather.18.cloned.1.call-update) | async-done | bytes 23068688 | tf_op jit(solution)/shard_map/all_gather | solution.py:124
  570.3 12.0 fusion.178
  582.3 132.9 %all-gather.20.cloned.1.call-done = bf16[5632,2048]{1,0:T(8,128)(2,1)} async-done(((bf16[176,2048]{1,0:T(8,128)(2,1)}), bf16[5632,2048]{1,0:T(8,128)(2,1)}) %all-gather.20.cloned.1.call-update) | async-done | bytes 23068688 | tf_op jit(solution)/shard_map/all_gather | solution.py:125
  715.2 15.7 multiply_convert_fusion.2
  730.9 14.0 fusion.181
  744.9 14.7 multiply_reduce_fusion.1
  759.6 12.5 fusion.180
  772.2 12.2 fusion.179
  784.4 22.3 multiply_convert_fusion
  806.7 14.0 fusion.183
  820.6 14.7 multiply_reduce_fusion
  835.3 5.2 fusion.167
  841.4 7.3 convolution_convert_fusion.1
  848.8 1.4 copy.62
  850.3 4.1 fusion.117
  854.4 3.8 fusion.5
  858.5 2.9 convolution_convert_fusion
  861.9 4.3 fusion.114
  866.9 2.2 fusion.126
  869.4 6.4 fusion.7
  877.0 6.7 fusion.2
  883.7 4.6 fusion.4
  891.4 2.1 fusion.127
  893.6 12.3 fusion.80
  909.6 1.5 copy-done.1
  914.9 8.3 fusion.76
  924.3 23.3 fusion.14
  948.1 23.3 fusion.10
  972.5 23.4 fusion.18
  996.0 6.4 fusion.182
  1003.0 6.3 fusion.184
  1012.1 2.0 fusion.62
  1014.1 38.9 %all-reduce.6 = (f32[2048]{0:T(1024)S(1)}, f32[2048]{0:T(1024)S(1)}) all-reduce(f32[2048]{0:T(1024)S(1)} %add.174, f32[2048]{0:T(1024)S(1)} %add.175), channel_id=9, replica_groups=mesh['dp'=4,'fsdp'=8] {'dp','fsdp'}, use_global_device_ids=true, to_apply=%region_27.28.clone | all-reduce | flops 4096 | bytes 32768
  1054.2 13.1 fusion.35
  1067.3 10.7 fusion.34
  1081.4 1.9 pad_maximum_fusion
  1083.3 59.9 %reduce-scatter.10.cloned.1.call-done = f32[64,256]{1,0:T(8,128)} async-done(((f32[2048,256]{1,0:T(8,128)}), f32[64,256]{1,0:T(8,128)}) %reduce-scatter.10.cloned.1.call-update) | async-done | bytes 65552 | tf_op jit(solution)/shard_map/reduce_scatter | solution.py:214
  1143.2 181.5 %reduce-scatter.14.cloned.1.call-done = f32[64,2048]{1,0:T(8,128)} async-done(((f32[2048,2048]{1,0:T(8,128)}), f32[64,2048]{1,0:T(8,128)}) %reduce-scatter.14.cloned.1.call-update) | async-done | bytes 524304 | tf_op jit(solution)/shard_map/reduce_scatter | solution.py:216
  1324.7 187.5 %reduce-scatter.8.cloned.1.call-done = f32[64,2048]{1,0:T(8,128)} async-done(((f32[2048,2048]{1,0:T(8,128)}), f32[64,2048]{1,0:T(8,128)}) %reduce-scatter.8.cloned.1.call-update) | async-done | bytes 524304 | tf_op jit(solution)/shard_map/reduce_scatter | solution.py:213
  1512.2 489.5 %reduce-scatter.18.cloned.1.call-done = f32[64,5632]{1,0:T(8,128)} async-done(((f32[2048,5632]{1,0:T(8,128)}), f32[64,5632]{1,0:T(8,128)}) %reduce-scatter.18.cloned.1.call-update) | async-done | bytes 1441808 | tf_op jit(solution)/shard_map/reduce_scatter | solution.py:203
  2001.8 496.1 %reduce-scatter.16.cloned.1.call-done = f32[64,5632]{1,0:T(8,128)} async-done(((f32[2048,5632]{1,0:T(8,128)}), f32[64,5632]{1,0:T(8,128)}) %reduce-scatter.16.cloned.1.call-update) | async-done | bytes 1441808 | tf_op jit(solution)/shard_map/reduce_scatter | solution.py:202
  2497.9 496.0 %reduce-scatter.20.cloned.1.call-done = f32[176,2048]{1,0:T(8,128)} async-done(((f32[5632,2048]{1,0:T(8,128)}), f32[176,2048]{1,0:T(8,128)}) %reduce-scatter.20.cloned.1.call-update) | async-done | bytes 1441808 | tf_op jit(solution)/shard_map/reduce_scatter | solution.py:204
  (298 shorter events, 41.3 us)
Async XLA Ops:
  7.2 4.8 copy-start.70
  7.2 7.7 copy-start.87
  7.2 7.9 copy-start.88
  7.2 50.4 %copy-start.86 = (s32[2,1]{0,1:T(1,128)S(1)}, s32[2,1]{0,1:T(1,128)}, u32[]{:S(2)}) copy-start(s32[2,1]{0,1:T(1,128)} %param.15) | copy-start | bytes 28
  7.2 54.4 %copy-start.2 = (bf16[2,192,2048]{2,1,0:T(8,128)(2,1)S(1)}, bf16[2,192,2048]{2,1,0:T(8,128)(2,1)}, u32[]{:S(2)}) copy-start(bf16[2,192,2048]{2,1,0:T(8,128)(2,1)} %param.13) | copy-start | bytes 4718596
  7.2 60.1 %all-gather.10.cloned.1.call-start = ((), (), s32[]{:S(2)}) async-start(), calls=%async_computation.8 | async-start | bytes 1081344 | tf_op jit(solution)/shard_map/all_gather | solution.py:95
  8.0 115.0 %all-gather.8.cloned.1.call-start = ((), (), s32[]{:S(2)}) async-start(), calls=%async_computation.7 | async-start | bytes 1081344 | tf_op jit(solution)/shard_map/all_gather | solution.py:96
  8.7 193.2 %all-gather.12.cloned.1.call-start = ((), (), s32[]{:S(2)}) async-start(), calls=%async_computation.9 | async-start | bytes 8650752 | tf_op jit(solution)/shard_map/all_gather | solution.py:94
  9.4 270.9 %all-gather.14.cloned.1.call-start = ((), (), s32[]{:S(2)}) async-start(), calls=%async_computation.10 | async-start | bytes 8650752 | tf_op jit(solution)/shard_map/all_gather | solution.py:97
  10.0 415.5 %all-gather.16.cloned.1.call-start = ((), (), s32[]{:S(2)}) async-start(), calls=%async_computation.11 | async-start | bytes 23789568 | tf_op jit(solution)/shard_map/all_gather | solution.py:123
  10.6 52.8 %copy-start.25 = (bf16[2,192,2048]{2,1,0:T(8,128)(2,1)S(1)}, bf16[2,192,2048]{2,1,0:T(8,128)(2,1)}, u32[]{:S(2)}) copy-start(bf16[2,192,2048]{2,1,0:T(8,128)(2,1)} %param.25) | copy-start | bytes 4718596
  10.6 559.7 %all-gather.18.cloned.1.call-start = ((), (), s32[]{:S(2)}) async-start(), calls=%async_computation.12 | async-start | bytes 23789568 | tf_op jit(solution)/shard_map/all_gather | solution.py:124
  11.2 704.0 %all-gather.20.cloned.1.call-start = ((), (), s32[]{:S(2)}) async-start(), calls=%async_computation.13 | async-start | bytes 23789568 | tf_op jit(solution)/shard_map/all_gather | solution.py:125
  11.9 1071.3 %reduce-scatter.12.cloned.1.call-start = ((), (), s32[]{:S(2)}) async-start(), calls=%async_computation.16 | async-start | bytes 2162688 | tf_op jit(solution)/shard_map/reduce_scatter | solution.py:215
  57.6 228.4 %copy-start.64 = (f32[2048]{0:T(1024)}, f32[2048]{0:T(1024)S(1)}, u32[]{:S(2)}) copy-start(f32[2048]{0:T(1024)S(1)} %convert_element_type.216) | copy-start | bytes 24580
  59.5 5.5 copy-start.71
  59.5 5.4 copy-start.74
  60.9 159.5 %copy-start.41 = (f32[192,64]{0,1:T(8,128)}, f32[192,64]{0,1:T(8,128)S(1)}, u32[]{:S(2)}) copy-start(f32[192,64]{0,1:T(8,128)S(1)} %get-tuple-element.105) | copy-start | bytes 147460
  60.9 231.9 %copy-start.39 = (f32[192,64]{0,1:T(8,128)}, f32[192,64]{0,1:T(8,128)S(1)}, u32[]{:S(2)}) copy-start(f32[192,64]{0,1:T(8,128)S(1)} %get-tuple-element.66) | copy-start | bytes 147460
  62.0 65.7 %copy-start.81 = (f32[192]{0:T(256)}, f32[192]{0:T(256)S(1)}, u32[]{:S(2)}) copy-start(f32[192]{0:T(256)S(1)} %get-tuple-element.104) | copy-start | bytes 2308
  65.4 60.0 %copy-start.4 = (bf16[192,2048]{1,0:T(8,128)(2,1)}, bf16[192,2048]{1,0:T(8,128)(2,1)S(1)}, u32[]{:S(2)}) copy-start(bf16[192,2048]{1,0:T(8,128)(2,1)S(1)} %get-tuple-element.49) | copy-start | bytes 2359300
  65.4 60.0 %copy-start.8 = (bf16[192,2048]{1,0:T(8,128)(2,1)}, bf16[192,2048]{1,0:T(8,128)(2,1)S(1)}, u32[]{:S(2)}) copy-start(bf16[192,2048]{1,0:T(8,128)(2,1)S(1)} %get-tuple-element.50) | copy-start | bytes 2359300
  130.2 90.7 %copy-start.48 = (bf16[192,4,64,1]{0,2,3,1:T(8,128)(2,1)}, bf16[192,4,64,1]{0,2,3,1:T(8,128)(2,1)S(1)}, u32[]{:S(2)}) copy-start(bf16[192,4,64,1]{0,2,3,1:T(8,128)(2,1)S(1)} %fusion.145) | copy-start | bytes 294916
  130.2 164.0 %copy-start.46 = (bf16[192,4,64,1]{0,2,3,1:T(8,128)(2,1)}, bf16[192,4,64,1]{0,2,3,1:T(8,128)(2,1)S(1)}, u32[]{:S(2)}) copy-start(bf16[192,4,64,1]{0,2,3,1:T(8,128)(2,1)S(1)} %fusion.144) | copy-start | bytes 294916
  201.9 12.4 copy-start.82
  220.9 5.3 copy-start.18
  221.2 5.0 copy-start.62
  280.3 5.7 copy-start.79
  286.0 549.3 %copy-start.12 = (f32[192,2048]{1,0:T(8,128)}, f32[192,2048]{1,0:T(8,128)S(1)}, u32[]{:S(2)}) copy-start(f32[192,2048]{1,0:T(8,128)S(1)} %get-tuple-element.89) | copy-start | bytes 4718596
  294.3 6.4 copy-start.60
  304.2 6.8 copy-start.28
  311.2 259.1 %copy-start.16 = (bf16[192,2048]{1,0:T(8,128)(2,1)}, bf16[192,2048]{1,0:T(8,128)(2,1)S(1)}, u32[]{:S(2)}) copy-start(bf16[192,2048]{1,0:T(8,128)(2,1)S(1)} %multiply_convert_fusion.7) | copy-start | bytes 2359300
  437.6 277.6 %copy-start.32 = (bf16[192,2048]{1,0:T(8,128)(2,1)S(1)}, bf16[192,2048]{1,0:T(8,128)(2,1)}, u32[]{:S(2)}) copy-start(bf16[192,2048]{1,0:T(8,128)(2,1)} %get-tuple-element.51) | copy-start | bytes 2359300
  730.9 14.0 copy-start.35
  730.9 14.0 copy-start.21
  759.6 12.5 copy-start.29
  772.2 12.2 copy-start.34
  806.7 14.0 copy-start.36
  820.6 14.7 copy-start.72
  820.6 14.7 copy-start.75
  841.4 8.8 copy-start.69
  841.4 12.9 slice-start.2
  850.2 7.9 slice-start
  854.4 11.9 copy-start.58
  861.9 5.0 copy-start.5
  861.9 5.0 copy-start.9
  869.1 274.0 %reduce-scatter.10.cloned.1.call-start = ((), (), s32[]{:S(2)}) async-start(), calls=%async_computation.15 | async-start | bytes 2162688 | tf_op jit(solution)/shard_map/reduce_scatter | solution.py:214
  869.3 6.4 copy-start.19
  876.9 6.7 slice-start.4
  877.0 6.7 slice-start.5
  883.7 4.6 copy-start.20
  893.5 431.2 %reduce-scatter.14.cloned.1.call-start = ((), (), s32[]{:S(2)}) async-start(), calls=%async_computation.17 | async-start | bytes 17301504 | tf_op jit(solution)/shard_map/reduce_scatter | solution.py:216
  905.9 606.3 %reduce-scatter.8.cloned.1.call-start = ((), (), s32[]{:S(2)}) async-start(), calls=%async_computation.14 | async-start | bytes 17301504 | tf_op jit(solution)/shard_map/reduce_scatter | solution.py:213
  923.2 1078.5 %reduce-scatter.18.cloned.1.call-start = ((), (), s32[]{:S(2)}) async-start(), calls=%async_computation.19 | async-start | bytes 47579136 | tf_op jit(solution)/shard_map/reduce_scatter | solution.py:203
  947.6 1550.2 %reduce-scatter.16.cloned.1.call-start = ((), (), s32[]{:S(2)}) async-start(), calls=%async_computation.18 | async-start | bytes 47579136 | tf_op jit(solution)/shard_map/reduce_scatter | solution.py:202
  971.4 2022.4 %reduce-scatter.20.cloned.1.call-start = ((), (), s32[]{:S(2)}) async-start(), calls=%async_computation.20 | async-start | bytes 47579136 | tf_op jit(solution)/shard_map/reduce_scatter | solution.py:204
  996.0 6.4 copy-start.15
  1012.0 42.1 %copy-start.13 = (f32[192,2048]{1,0:T(8,128)S(1)}, f32[192,2048]{1,0:T(8,128)}, u32[]{:S(2)}) copy-start(f32[192,2048]{1,0:T(8,128)} %copy-done.12) | copy-start | bytes 4718596
  1012.0 42.1 %copy-start.76 = (f32[192]{0:T(256)S(1)}, f32[192]{0:T(256)}, u32[]{:S(2)}) copy-start(f32[192]{0:T(256)} %copy-done.74) | copy-start | bytes 2308
  1054.2 13.1 copy-start.22
  1054.2 13.1 copy-start.37
  1054.2 13.1 copy-start.73
  1067.3 12.0 copy-start.27
  1067.3 12.0 copy-start.38
  (45 other events, 83.0 us)
Sparse Core Ops, SparseCore 0:
  10.9 56.4 all-gather.9
  70.2 52.6 all-gather.7
  125.8 76.0 all-gather.11
  204.6 75.6 all-gather.13
  283.0 142.4 all-gather.15
  428.2 142.0 all-gather.17
  573.1 142.0 all-gather.19
  869.2 136.5 reduce-scatter.11
  1008.7 134.4 reduce-scatter.9
  1145.9 178.7 reduce-scatter.13
  1327.6 184.6 reduce-scatter.7
  1515.0 486.7 reduce-scatter.17
  2004.6 493.1 reduce-scatter.15
  2500.6 493.1 reduce-scatter.19
where the time goes:
time: 3010 us; the launch traced here: 3000 us
  waiting for transfers between devices  2470 us (82%)
  matrix products  362 us (12%)
  blocking collectives  81 us (3%)
  local copies, waits for them, and re-layouts  35.9 us (1%)
  other arithmetic  32.4 us (1%)
    reduce_scatter x1, waiting for transfers between devices, local(): lax.psum_scatter(grad_wg, ('dp', 'fsdp'), scatter_dimension=0, tiled=True)  496 us
    reduce_scatter x1, waiting for transfers between devices, local(): lax.psum_scatter(grad_wd, ('dp', 'fsdp'), scatter_dimension=0, tiled=True)  496 us
    reduce_scatter x1, waiting for transfers between devices, local(): lax.psum_scatter(grad_wu, ('dp', 'fsdp'), scatter_dimension=0, tiled=True)  490 us
    reduce_scatter x1, waiting for transfers between devices, local(): lax.psum_scatter(grad_wq, ('dp', 'fsdp'), scatter_dimension=0, tiled=True)  188 us
    reduce_scatter x1, waiting for transfers between devices, local(): lax.psum_scatter(grad_wo, ('dp', 'fsdp'), scatter_dimension=0, tiled=True)  182 us
    all_gather x1, waiting for transfers between devices, local(): lax.all_gather(w_down, ('dp', 'fsdp'), axis=0, tiled=True)  133 us
    all_gather x1, waiting for transfers between devices, local(): lax.all_gather(w_up, ('dp', 'fsdp'), axis=0, tiled=True)  133 us
    dot_general x14, matrix products, against(): lax.dot_general(left, weight, (((1,), (1,)), ((), ())), preferred_element...  122 us
  transfers between devices with their start and end apart: 14, of which 13 were waited for; matrix products, arithmetic and copies ran while one was open for 9% of the time, Pallas kernels for 0%

commit v1 on v0

v1 whole, which is shorter than its diff:
```python
import jax
import jax.numpy as jnp
from jax import lax
from jax.experimental import pallas as pl
from jax.experimental.pallas import tpu as pltpu
from jax.sharding import Mesh, PartitionSpec as P

HEADS = 32
KV_HEADS = 4
HEAD_DIM = 64
MICRO = 2
RANKS = 4
SCALING = HEAD_DIM ** (-0.5)
EPS = 1e-05
NEG = -1000000000.0
BF16 = jnp.bfloat16
F32 = jnp.float32


def contract(left, right, dims):
    return lax.dot_general(left, right, (dims, ((), ())), preferred_element_type=F32)


def inner_rows(left, right):
    return contract(left, right, ((0,), (0,)))


def against(left, weight):
    return contract(left, weight, ((1,), (1,)))


def forward_dot(left, weight):
    return contract(left, weight, ((1,), (0,)))


def turned_half(value):
    lane = lax.broadcasted_iota(jnp.int32, value.shape, 1)
    width = value.shape[1]
    ahead = pltpu.roll(value, width - HEAD_DIM // 2, axis=1)
    behind = pltpu.roll(value, HEAD_DIM // 2, axis=1)
    return jnp.where(lane % HEAD_DIM < HEAD_DIM // 2, -ahead, behind)


def stacked_heads(pair):
    return jnp.concatenate([pair[:, :HEAD_DIM], pair[:, HEAD_DIM:]], axis=0)


def paired_heads(tall):
    rows = tall.shape[0] // 2
    return jnp.concatenate([tall[:rows], tall[rows:]], axis=1)


def allowed_pairs(segc_ref, segr_ref):
    segc, segr = segc_ref[0], segr_ref[0]
    rows = segc.shape[0]
    later = lax.broadcasted_iota(jnp.int32, (rows, rows), 0)
    earlier = lax.broadcasted_iota(jnp.int32, (rows, rows), 1)
    allow = jnp.logical_and(segc == segr, earlier <= later)
    return jnp.where(allow, 0.0, NEG)


def head_probs(tall_q, key, bias):
    scores = contract(tall_q, key, ((1,), (1,))) * SCALING
    rows = bias.shape[0]
    scores = jnp.concatenate(
        [
            jnp.where(bias < 0.0, bias, scores[:rows]),
            jnp.where(bias < 0.0, bias, scores[rows:]),
        ],
        axis=0,
    )
    top = jnp.max(scores, axis=1, keepdims=True)
    grown = jnp.exp(scores - top)
    return grown / jnp.sum(grown, axis=1, keepdims=True)


def attend_kernel(width, side, qkv_ref, tab_ref, segc_ref, segr_ref, o_ref, qr_ref, kr_ref, v_ref):
    cos_t, sin_t = tab_ref[:, :128], tab_ref[:, 128:]
    bias = allowed_pairs(segc_ref, segr_ref)
    kinds = []
    for start in range(0, side, 128):
        piece = qkv_ref[:, width + start : width + start + 128]
        piece = (piece * cos_t + turned_half(piece) * sin_t).astype(BF16)
        kr_ref[:, start : start + 128] = piece
        kinds.append(piece)
    values = qkv_ref[:, width + side :].astype(BF16)
    v_ref[...] = values
    for group in range(width // 128):
        piece = qkv_ref[:, group * 128 : group * 128 + 128]
        piece = (piece * cos_t + turned_half(piece) * sin_t).astype(BF16)
        qr_ref[:, group * 128 : group * 128 + 128] = piece
        at = (group % 2) * HEAD_DIM
        key = kinds[group // 2][:, at : at + HEAD_DIM]
        probs = head_probs(stacked_heads(piece), key, bias)
        value = values[:, group * HEAD_DIM : group * HEAD_DIM + HEAD_DIM]
        mixed = contract(probs.astype(BF16), value, ((1,), (0,)))
        o_ref[:, group * 128 : group * 128 + 128] = paired_heads(mixed).astype(BF16)


def attend_back_kernel(
    width, side, do_ref, qr_ref, kr_ref, v_ref, tab_ref, segc_ref, segr_ref, out_ref
):
    cos_t, sin_t = tab_ref[:, :128], tab_ref[:, 128:]
    bias = allowed_pairs(segc_ref, segr_ref)
    key_grads = []
    value_grads = []
    for group in range(width // 128):
        tall_q = stacked_heads(qr_ref[:, group * 128 : group * 128 + 128])
        tall_do = stacked_heads(do_ref[:, group * 128 : group * 128 + 128])
        here = slice(group * HEAD_DIM, group * HEAD_DIM + HEAD_DIM)
        key, value = kr_ref[:, here], v_ref[:, here]
        probs = head_probs(tall_q, key, bias)
        value_grads.append(contract(probs.astype(BF16), tall_do, ((0,), (0,))))
        grad_probs = contract(tall_do, value, ((1,), (1,)))
        kept = jnp.sum(grad_probs * probs, axis=1, keepdims=True)
        grad_scores = (probs * (grad_probs - kept)).astype(BF16)
        grad_q = paired_heads(contract(grad_scores, key, ((1,), (0,)))) * SCALING
        grad_q = grad_q * cos_t - turned_half(grad_q) * sin_t
        out_ref[:, group * 128 : group * 128 + 128] = grad_q.astype(BF16)
        key_grads.append(contract(grad_scores, tall_q, ((0,), (0,))) * SCALING)
    for index in range(side // 128):
        both = jnp.concatenate([key_grads[2 * index], key_grads[2 * index + 1]], axis=1)
        both = both * cos_t - turned_half(both) * sin_t
        at = width + index * 128
        out_ref[:, at : at + 128] = both.astype(BF16)
        both = jnp.concatenate([value_grads[2 * index], value_grads[2 * index + 1]], axis=1)
        at = width + side + index * 128
        out_ref[:, at : at + 128] = both.astype(BF16)


def rows_spec(rows, columns):
    return pl.BlockSpec((rows, columns), lambda block: (block, 0))


def segment_specs(rows):
    return [
        pl.BlockSpec((1, rows, 1), lambda block: (block, 0, 0)),
        pl.BlockSpec((1, 1, rows), lambda block: (block, 0, 0)),
    ]


def attend(qkv, table, segments, width, side):
    blocks, rows = segments.shape

    def kernel(*refs):
        attend_kernel(width, side, *refs)

    return pl.pallas_call(
        kernel,
        grid=(blocks,),
        in_specs=[rows_spec(rows, qkv.shape[1]), rows_spec(rows, 256)] + segment_specs(rows),
        out_specs=[
            rows_spec(rows, width),
            rows_spec(rows, width),
            rows_spec(rows, side),
            rows_spec(rows, side),
        ],
        out_shape=[
            jax.ShapeDtypeStruct((blocks * rows, columns), BF16)
            for columns in (width, width, side, side)
        ],
        name="attend",
    )(qkv, table, segments[:, :, None], segments[:, None, :])


def attend_back(grad_mixed, q_rot, k_rot, values, table, segments, width, side):
    blocks, rows = segments.shape

    def kernel(*refs):
        attend_back_kernel(width, side, *refs)

    return pl.pallas_call(
        kernel,
        grid=(blocks,),
        in_specs=[
            rows_spec(rows, width),
            rows_spec(rows, width),
            rows_spec(rows, side),
            rows_spec(rows, side),
            rows_spec(rows, 256),
        ]
        + segment_specs(rows),
        out_specs=rows_spec(rows, width + 2 * side),
        out_shape=jax.ShapeDtypeStruct((blocks * rows, width + 2 * side), BF16),
        name="attend_back",
    )(grad_mixed, q_rot, k_rot, values, table, segments[:, :, None], segments[:, None, :])


def rope_table(segments):
    rows = segments.shape[1]
    span = jnp.arange(rows, dtype=jnp.int32)
    same = (segments[:, :, None] == segments[:, None, :]) & (span[None, :] < span[:, None])
    pos = jnp.sum(same.astype(jnp.int32), axis=2).reshape(-1)
    steps = jnp.arange(HEAD_DIM // 2, dtype=jnp.int32).astype(F32)
    freq = 10000.0 ** (-2.0 * steps / HEAD_DIM)
    angle = pos.astype(F32)[:, None] * freq[None, :]
    cos_half, sin_half = jnp.cos(angle), jnp.sin(angle)
    return jnp.concatenate([cos_half] * 4 + [sin_half] * 4, axis=1)


def swap(value, axis):
    return lax.ppermute(value, axis, [(0, 1), (1, 0)])


def gather_group(value):
    across = swap(value, "x")
    beside = swap(value, "c")
    beside_across = swap(across, "c")
    return jnp.concatenate([value, across, beside, beside_across], axis=0)


def reduce_group(product, left):
    quarter = left.shape[0] // RANKS
    far = product(left[2 * quarter :]).astype(BF16)
    from_core = swap(far, "c")
    across = product(left[quarter : 2 * quarter]) + from_core[quarter:].astype(F32)
    from_chip = swap(across.astype(BF16), "x")
    own = product(left[:quarter]) + from_core[:quarter].astype(F32)
    return own + from_chip.astype(F32)


def gather_rows(value):
    return lax.all_gather(value, ("dp", "y"), axis=0, tiled=True)


def scatter_rows(value):
    return lax.psum_scatter(value, ("dp", "y"), scatter_dimension=0, tiled=True)


def exchange(value):
    return lax.all_to_all(value, ("x", "c"), 0, 0, tiled=True)


def by_rank(weight, piece):
    rows, columns = weight.shape
    parts = weight.reshape(rows, columns // (RANKS * piece), RANKS, piece)
    return parts.transpose(2, 0, 1, 3).reshape(RANKS * rows, columns // RANKS)


def from_ranks(value, piece):
    ranks, rows, columns = value.shape
    parts = value.reshape(ranks, rows, columns // piece, piece)
    return parts.transpose(1, 2, 0, 3).reshape(rows, ranks * columns)


def unit(value):
    scale = lax.rsqrt(jnp.mean(value * value, axis=-1, keepdims=True) + EPS)
    return value * scale, scale


def unit_back(normed, scale, grad):
    return scale * (grad - normed * jnp.mean(grad * normed, axis=-1, keepdims=True))


def layer(
    layer_input,
    segment_ids,
    live_counts,
    w_query,
    w_key,
    w_value,
    w_out,
    w_gate,
    w_up,
    w_down,
    attn_gain,
    mlp_gain,
    out_grad,
):
    micro, rows, model = layer_input.shape
    tokens = micro * rows
    owned = w_query.shape[0]
    piece = w_down.shape[0]
    width = w_query.shape[1] // RANKS
    side = w_key.shape[1]
    hidden_units = w_gate.shape[1] // RANKS
    span = jnp.arange(rows, dtype=jnp.int32)
    valid = (span[None, :] < live_counts).astype(F32).reshape(tokens, 1)

    gain1 = attn_gain.astype(F32)[:, None]
    gain2 = mlp_gain.astype(F32)[:, None]
    scaled = lambda weight, gain: (weight.astype(F32) * gain).astype(BF16)
    side_weights = jnp.concatenate([scaled(w_key, gain1), scaled(w_value, gain1)], axis=1)
    qkv_sent = jnp.concatenate(
        [by_rank(scaled(w_query, gain1), HEAD_DIM), jnp.tile(side_weights, (RANKS, 1))], axis=1
    )
    gu_sent = jnp.concatenate(
        [by_rank(scaled(w_gate, gain2), piece), by_rank(scaled(w_up, gain2), piece)], axis=1
    )
    w_qkv = gather_rows(exchange(qkv_sent))
    wo = gather_rows(w_out)
    w_gu = gather_rows(exchange(gu_sent))
    wd = gather_rows(w_down)

    segments = gather_group(segment_ids)
    table = rope_table(segments)

    inputs = layer_input.reshape(tokens, model).astype(F32)
    n1, r1 = unit(inputs)
    n1_all = gather_group(n1.astype(BF16))
    error = out_grad.reshape(tokens, model).astype(F32) * valid
    error_all = gather_group(error.astype(BF16))

    qkv = forward_dot(n1_all, w_qkv)
    mixed, q_rot, k_rot, values = attend(qkv, table, segments, width, side)
    hidden = inputs + reduce_group(lambda left: forward_dot(left, wo), mixed)

    n2, r2 = unit(hidden)
    n2_all = gather_group(n2.astype(BF16))
    gate_up = forward_dot(n2_all, w_gu)
    gate, upward = gate_up[:, :hidden_units], gate_up[:, hidden_units:]
    sigma = jax.nn.sigmoid(gate)
    silu_gate = gate * sigma
    inner = (silu_gate * upward).astype(BF16)
    result = hidden + reduce_group(lambda left: forward_dot(left, wd), inner)
    layer_output = (result * valid).astype(BF16).reshape(micro, rows, model)

    grad_wd = scatter_rows(inner_rows(inner, error_all).astype(BF16)).astype(F32)
    grad_inner = against(error_all, wd)
    grad_gate = grad_inner * upward * (sigma + gate * sigma * (1.0 - sigma))
    grad_up = grad_inner * silu_gate
    grad_gu = jnp.concatenate([grad_gate.astype(BF16), grad_up.astype(BF16)], axis=1)
    gu_raw = exchange(scatter_rows(inner_rows(n2_all, grad_gu).astype(BF16)))
    grad_n2 = reduce_group(lambda left: against(left, w_gu), grad_gu)
    grad_hidden = error + unit_back(n2, r2, grad_n2)
    hidden_all = gather_group(grad_hidden.astype(BF16))
    grad_mixed = against(hidden_all, wo).astype(BF16)
    grad_wo = scatter_rows(inner_rows(mixed, hidden_all).astype(BF16)).astype(F32)
    grad_qkv = attend_back(grad_mixed, q_rot, k_rot, values, table, segments, width, side)
    qkv_raw = exchange(scatter_rows(inner_rows(n1_all, grad_qkv).astype(BF16)))
    grad_n1 = reduce_group(lambda left: against(left, w_qkv), grad_qkv)
    input_grad = (grad_hidden + unit_back(n1, r1, grad_n1)).reshape(micro, rows, model)

    gu_raw = gu_raw.reshape(RANKS, owned, 2 * hidden_units).astype(F32)
    raw_gate = from_ranks(gu_raw[:, :, :hidden_units], piece)
    raw_up = from_ranks(gu_raw[:, :, hidden_units:], piece)
    qkv_raw = qkv_raw.reshape(RANKS, owned, width + 2 * side).astype(F32)
    raw_query = from_ranks(qkv_raw[:, :, :width], HEAD_DIM)
    raw_side = jnp.sum(qkv_raw[:, :, width:], axis=0)
    raw_key, raw_value = raw_side[:, :side], raw_side[:, side:]
    row_dot = lambda raw, weight: jnp.sum(raw * weight.astype(F32), axis=1)
    grad_gain1 = row_dot(raw_query, w_query) + row_dot(raw_key, w_key) + row_dot(raw_value, w_value)
    grad_gain2 = row_dot(raw_gate, w_gate) + row_dot(raw_up, w_up)
    return (
        layer_output,
        input_grad,
        raw_query * gain1,
        raw_key * gain1,
        raw_value * gain1,
        grad_wo,
        raw_gate * gain2,
        raw_up * gain2,
        grad_wd,
        grad_gain1,
        grad_gain2,
    )


def positions(segment):
    place = jnp.arange(segment.shape[0], dtype=jnp.int32)
    before = jnp.concatenate([segment[:1] - 1, segment[:-1]])
    start = lax.cummax(jnp.where(segment != before, place, 0), axis=0)
    return place - start


def rope_pair(pos):
    steps = jnp.arange(HEAD_DIM // 2, dtype=jnp.int32).astype(F32)
    freq = 10000.0 ** (-2.0 * steps / HEAD_DIM)
    angle = pos.astype(F32)[:, None] * freq[None, :]
    cos_half, sin_half = jnp.cos(angle), jnp.sin(angle)
    return (
        jnp.concatenate([cos_half, cos_half], axis=-1),
        jnp.concatenate([sin_half, sin_half], axis=-1),
    )


def rotate(value, cos_t, sin_t):
    half = HEAD_DIM // 2
    turned = jnp.concatenate([-value[..., half:], value[..., :half]], axis=-1)
    return value * cos_t[:, None, :] + turned * sin_t[:, None, :]


def plain_layer(
    layer_input,
    segment_ids,
    live_counts,
    w_query,
    w_key,
    w_value,
    w_out,
    w_gate,
    w_up,
    w_down,
    attn_gain,
    mlp_gain,
    out_grad,
):
    axes = ("dp", "y", "x", "c")
    rows = layer_input.shape[1]
    group = HEADS // KV_HEADS
    width = HEADS * HEAD_DIM
    span = jnp.arange(rows, dtype=jnp.int32)
    whole = lambda value: lax.all_gather(value, axes, axis=0, tiled=True)
    wq, wk, wv, wo, g1 = [whole(w) for w in (w_query, w_key, w_value, w_out, attn_gain)]
    wg, wu, wd, g2 = [whole(w) for w in (w_gate, w_up, w_down, mlp_gain)]
    gain1, gain2 = g1.astype(F32), g2.astype(F32)
    outputs, input_grads, kept = [], [], []
    gain_sums = [0.0, 0.0]
    for micro in range(MICRO):
        segment = segment_ids[micro]
        valid = (span < live_counts[micro, 0]).astype(F32)[:, None]
        cos_t, sin_t = rope_pair(positions(segment))
        allow = (segment[:, None] == segment[None, :]) & (span[None, :] <= span[:, None])
        inputs = layer_input[micro].astype(F32)
        n1, r1 = unit(inputs)
        h1 = (n1 * gain1).astype(BF16)
        query = forward_dot(h1, wq).reshape(rows, HEADS, HEAD_DIM)
        keys = forward_dot(h1, wk).reshape(rows, KV_HEADS, HEAD_DIM)
        values = forward_dot(h1, wv).astype(BF16).reshape(rows, KV_HEADS, HEAD_DIM)
        q_rot = rotate(query, cos_t, sin_t).astype(BF16).reshape(rows, KV_HEADS, group, HEAD_DIM)
        k_rot = rotate(keys, cos_t, sin_t).astype(BF16)
        scores = jnp.einsum("qkgd,skd->kgqs", q_rot, k_rot, preferred_element_type=F32) * SCALING
        probs = jax.nn.softmax(jnp.where(allow, scores, NEG), axis=-1)
        probs_b = probs.astype(BF16)
        mixed = jnp.einsum("kgqs,skd->qkgd", probs_b, values, preferred_element_type=F32)
        mixed = mixed.reshape(rows, width).astype(BF16)
        hidden = inputs + forward_dot(mixed, wo)
        n2, r2 = unit(hidden)
        h2 = (n2 * gain2).astype(BF16)
        gate, upward = forward_dot(h2, wg), forward_dot(h2, wu)
        sigma = jax.nn.sigmoid(gate)
        inner = (gate * sigma * upward).astype(BF16)
        outputs.append(((hidden + forward_dot(inner, wd)) * valid).astype(BF16))
        error = out_grad[micro].astype(F32) * valid
        error_low = error.astype(BF16)
        grad_inner = against(error_low, wd)
        grad_gate = (grad_inner * upward * (sigma + gate * sigma * (1.0 - sigma))).astype(BF16)
        grad_up = (grad_inner * gate * sigma).astype(BF16)
        grad_h2 = against(grad_gate, wg) + against(grad_up, wu)
        gain_sums[1] += jnp.sum(n2 * grad_h2, axis=0)
        grad_hidden = error + unit_back(n2, r2, grad_h2 * gain2)
        grad_low = grad_hidden.astype(BF16)
        grad_mixed = against(grad_low, wo).astype(BF16).reshape(rows, KV_HEADS, group, HEAD_DIM)
        grad_probs = jnp.einsum("qkgd,skd->kgqs", grad_mixed, values, preferred_element_type=F32)
        kept_sum = jnp.sum(grad_probs * probs, axis=-1, keepdims=True)
        grad_scores = (probs * (grad_probs - kept_sum)).astype(BF16)
        grad_values = jnp.einsum("kgqs,qkgd->skd", probs_b, grad_mixed, preferred_element_type=F32)
        grad_values = grad_values.astype(BF16).reshape(rows, KV_HEADS * HEAD_DIM)
        grad_q = jnp.einsum("kgqs,skd->qkgd", grad_scores, k_rot, preferred_element_type=F32)
        grad_k = jnp.einsum("kgqs,qkgd->skd", grad_scores, q_rot, preferred_element_type=F32)
        grad_q = rotate(grad_q.reshape(rows, HEADS, HEAD_DIM) * SCALING, cos_t, -sin_t)
        grad_q = grad_q.astype(BF16).reshape(rows, width)
        grad_k = rotate(grad_k * SCALING, cos_t, -sin_t)
        grad_k = grad_k.astype(BF16).reshape(rows, KV_HEADS * HEAD_DIM)
        grad_h1 = against(grad_q, wq) + against(grad_k, wk) + against(grad_values, wv)
        gain_sums[0] += jnp.sum(n1 * grad_h1, axis=0)
        input_grads.append(grad_hidden + unit_back(n1, r1, grad_h1 * gain1))
        kept.append(
            (h1, grad_q, grad_k, grad_values, mixed, grad_low)
            + (h2, grad_gate, grad_up, inner, error_low)
        )
    joined = [jnp.concatenate(items, axis=0) for items in zip(*kept)]
    scatter = lambda value: lax.psum_scatter(value, axes, scatter_dimension=0, tiled=True)
    pairs = ((0, 1), (0, 2), (0, 3), (4, 5), (6, 7), (6, 8), (9, 10))
    grads = [scatter(inner_rows(joined[left], joined[right])) for left, right in pairs]
    return (
        jnp.stack(outputs, axis=0),
        jnp.stack(input_grads, axis=0),
        *grads,
        scatter(gain_sums[0]),
        scatter(gain_sums[1]),
    )


def solution(mesh):
    inner, outer = mesh.shape["fsdp"], mesh.shape["dp"]
    grid = Mesh(mesh.devices.reshape(outer, inner // RANKS, 2, 2), ("dp", "y", "x", "c"))
    every = ("dp", "y", "x", "c")
    tokens = P(None, every, None)
    flat = P(None, every)
    weight = P(every, None)
    gain = P(every)
    in_specs = (tokens, flat, flat) + (weight,) * 7 + (gain, gain, tokens)
    out_specs = (tokens, tokens) + (weight,) * 7 + (gain, gain)

    def step(*args):
        whole_heads = args[6].shape[0] == HEAD_DIM * mesh.size
        body = layer if whole_heads else plain_layer
        return jax.shard_map(
            body, mesh=grid, in_specs=in_specs, out_specs=out_specs, check_vma=False
        )(*args)

    return step
```

time: 3010 us -> 1010 us (0.34)
  waiting for transfers between devices: 2470 us -> 576 us
  matrix products: 362 us -> 224 us
  Pallas kernels: 0 us -> 55.1 us
  blocking collectives: 81 us -> 34.9 us
    reduce_scatter x7 -> x4, waiting for transfers between devices: 1910 us -> 242 us  [scatter_rows(): return lax.psum_scatter(value, ('dp', 'y'), scatter_dimension=0, tiled=True)]
    all_gather x7 -> x4, waiting for transfers between devices: 557 us -> 98.8 us  [gather_rows(): return lax.all_gather(value, ('dp', 'y'), axis=0, tiled=True)]
    ppermute x0 -> x23, waiting for transfers between devices: none -> 228 us  [swap(): return lax.ppermute(value, axis, [(0, 1), (1, 0)])]
    dot_general x45 -> x20, matrix products: 350 us -> 224 us  [contract(): lax.dot_general(left, right, (dims, ((), ())), preferred_element_type=F32)]
    unnamed x2 -> x0, blocking collectives: 81 us -> none
    pallas_call x0 -> x2, Pallas kernels: none -> 55.1 us  [the longest x1 32.1 us: attend_back(): pl.pallas_call(kernel, grid=(blocks,), in_specs=[rows_spec(rows, width),...]
    all_to_all x0 -> x2, blocking collectives: none -> 34.9 us  [exchange(): return lax.all_to_all(value, ('x', 'c'), 0, 0, tiled=True)]
  transfers between devices with their start and end apart: 14 -> 33, of which waited for: 13 -> 20; matrix products, arithmetic and copies ran while one was open for 9% -> 23% of each run, Pallas kernels for 0% -> 5%
where the time goes in v1:
time: 1010 us; the launch traced here: 1000 us
  waiting for transfers between devices  576 us (57%)
  matrix products  224 us (22%)
  Pallas kernels  55.1 us (5%)
  local copies, waits for them, and re-layouts  42.1 us (4%)
  other arithmetic  36.6 us (4%)
  blocking collectives  34.9 us (3%)
  starting transfers between devices  19.7 us (2%)
  between operations  15 us (1%)
    reduce_scatter x4, waiting for transfers between devices, scatter_rows(): return lax.psum_scatter(value, ('dp', 'y'), scatter_dimension=0, tiled=True)  242 us
    ppermute x23, waiting for transfers between devices, swap(): return lax.ppermute(value, axis, [(0, 1), (1, 0)])  228 us
    dot_general x20, matrix products, contract(): lax.dot_general(left, right, (dims, ((), ())), preferred_element_type=F32)  224 us
    all_gather x4, waiting for transfers between devices, gather_rows(): return lax.all_gather(value, ('dp', 'y'), axis=0, tiled=True)  98.8 us
    all_to_all x2, blocking collectives, exchange(): return lax.all_to_all(value, ('x', 'c'), 0, 0, tiled=True)  34.9 us
    pallas_call x1, Pallas kernels, attend_back(): pl.pallas_call(kernel, grid=(blocks,), in_specs=[rows_spec(rows, width),...  32.1 us
    pallas_call x1, Pallas kernels, attend(): pl.pallas_call(kernel, grid=(blocks,), in_specs=[rows_spec(rows, qkv.shap...  23 us
  transfers between devices with their start and end apart: 33, of which 20 were waited for; matrix products, arithmetic and copies ran while one was open for 23% of the time, Pallas kernels for 5%

profile of v1, /device:TPU:0, one launch (start us, length us, event | category | flops | bytes accessed | tf_op | source)
XLA Modules:
  0.0 1003.3 jit_solution(14294990192281167457)
XLA Ops:
  10.1 13.0 %all_to_all.36 = bf16[4,64,1024]{2,1,0:T(8,128)(2,1)} all-to-all(bf16[4,64,1024]{2,1,0:T(8,128)(2,1)S(1)} %pad_maximum_fusion.15), channel_id=1, replica_groups=mesh['dp'=4,'y'=2,'x'=2,'c'=2] {'x','c'}, dimensions={0} | all-to-all | bytes 1048576 | tf_op jit(solution)/shard_map/all_to_all | solution.py:231
  24.6 2.1 reshape.169
  27.9 2.1 reshape.170
  31.4 22.0 %all_to_all.37 = bf16[4,64,2816]{2,1,0:T(8,128)(2,1)} all-to-all(bf16[4,64,2816]{2,1,0:T(8,128)(2,1)S(1)} %pad_maximum_fusion.6), channel_id=1, replica_groups=mesh['dp'=4,'y'=2,'x'=2,'c'=2] {'x','c'}, dimensions={0} | all-to-all | bytes 2883584 | tf_op jit(solution)/shard_map/all_to_all | solution.py:231
  56.2 35.7 %collective-permute-done = bf16[384,2048]{1,0:T(8,128)(2,1)} collective-permute-done((bf16[384,2048]{1,0:T(8,128)(2,1)}, bf16[384,2048]{1,0:T(8,128)(2,1)}, u32[]{:S(2)}, u32[]{:S(2)}) %collective-permute-start) | collective-permute-done | bytes 1572896 | tf_op jit(solution)/shard_map/ppermute | solution.py:202
  93.0 2.5 collective-permute-done.3
  99.2 2.8 multiply_sine_fusion
  102.0 3.0 concatenate.43.refs_1_.refs_4_
  105.0 13.5 %fusion.37.refs_0_ = f32[1536,1024]{1,0:T(8,128)} fusion(bf16[2048,1024]{1,0:T(8,128)(2,1)} %all-gather.5.cloned.1.call-done, bf16[384,2048]{1,0:T(8,128)(2,1)} %collective-permute-done.2, bf16[384,2048]{1,0:T(8,128)(2,1)} %collective-permute-done.1, bf16[384,2048]{1,0:T(8,128)(2,1)} %collective-permute-done, bf16[384,2048]{1,0:T(8,128)(2,1)} %fusion.10), kind=kOutput, calls=%fused_computation.77 | convolution fusion | flops 6467616768 | bytes 16777216 | tf_op jit(solution)/shard_map/dot_general | solution.py:21
  118.5 23.0 %attend.1 = (bf16[1536,512]{1,0:T(8,128)(2,1)}, bf16[1536,512]{1,0:T(8,128)(2,1)}, bf16[1536,256]{1,0:T(8,128)(2,1)}, bf16[1536,256]{1,0:T(8,128)(2,1)}) custom-call(f32[1536,1024]{1,0:T(8,128)} %fusion.37.refs_0_, f32[1536,256]{1,0:T(8,128)} %concatenate.43.refs_1_.refs_4_, s32[8,192,1]{2,1,0:T(8,128)} %copy.53.refs_2_.refs_5_, ...), custom_call_target="tpu_custom_call" | custom-call | tf_op jit(solution)/shard_map/attend/pallas_call | solution.py:148
  141.5 5.1 all-gather.7.cloned.1.call-done
  146.6 5.4 convolution_convert_fusion.3
  152.1 5.9 collective-permute-done.6
  158.1 3.1 add_convert_fusion.3
  161.1 1.7 collective-permute-start.7
  163.8 33.9 %collective-permute-done.7 = bf16[384,2048]{1,0:T(8,128)(2,1)S(1)} collective-permute-done((bf16[384,2048]{1,0:T(8,128)(2,1)S(1)}, bf16[384,2048]{1,0:T(8,128)(2,1)S(1)}, u32[]{:S(2)}, u32[]{:S(2)}) %collective-permute-start.7) | collective-permute-done | bytes 1572896 | tf_op jit(solution)/shard_map/ppermute | solution.py:202
  197.7 2.4 multiply_reduce_fusion.1
  200.1 1.6 copy-done
  202.0 1.6 collective-permute-start.8
  205.7 33.7 %collective-permute-done.8 = bf16[384,2048]{1,0:T(8,128)(2,1)} collective-permute-done((bf16[384,2048]{1,0:T(8,128)(2,1)S(1)}, bf16[384,2048]{1,0:T(8,128)(2,1)}, u32[]{:S(2)}, u32[]{:S(2)}) %collective-permute-start.8) | collective-permute-done | bytes 1572896 | tf_op jit(solution)/shard_map/ppermute | solution.py:202
  239.9 31.7 %collective-permute-done.13 = bf16[384,2048]{1,0:T(8,128)(2,1)} collective-permute-done((bf16[384,2048]{1,0:T(8,128)(2,1)}, bf16[384,2048]{1,0:T(8,128)(2,1)}, u32[]{:S(2)}, u32[]{:S(2)}) %collective-permute-start.13) | collective-permute-done | bytes 1572896 | tf_op jit(solution)/shard_map/ppermute | solution.py:202
  271.7 39.1 %all-gather.9.cloned.1.call-done = bf16[2048,2816]{1,0:T(8,128)(2,1)} async-done(((bf16[256,2816]{1,0:T(8,128)(2,1)}), bf16[2048,2816]{1,0:T(8,128)(2,1)}) %all-gather.9.cloned.1.call-update) | async-done | bytes 11534352 | tf_op jit(solution)/shard_map/all_gather | solution.py:223
  310.7 37.9 %fusion.36 = f32[1536,2816]{1,0:T(8,128)} fusion(bf16[2048,2816]{1,0:T(8,128)(2,1)} %all-gather.9.cloned.1.call-done, bf16[384,2048]{1,0:T(8,128)(2,1)} %collective-permute-done.10, bf16[384,2048]{1,0:T(8,128)(2,1)S(1)} %collective-permute-done.9, bf16[384,2048]{1,0:T(8,128)(2,1)} %collective-permute-done.8, bf16[384,2048]{1,0:T(8,128)(2,1)S(1)} %multiply_convert_fusion.4), kind=kOutput, calls=%fused_computation.76 | convolution fusion | flops 17741905920 | bytes 35127296 | tf_op jit(solution)/shard_map/dot_general | solution.py:21
  348.7 54.6 %all-gather.11.cloned.1.call-done = bf16[1408,2048]{1,0:T(8,128)(2,1)} async-done(((bf16[176,2048]{1,0:T(8,128)(2,1)}), bf16[1408,2048]{1,0:T(8,128)(2,1)}) %all-gather.11.cloned.1.call-update) | async-done | bytes 5767184 | tf_op jit(solution)/shard_map/all_gather | solution.py:223
  403.3 22.5 %multiply_convert_fusion = (bf16[1536,1408]{1,0:T(8,128)(2,1)}, bf16[1536,1408]{1,0:T(8,128)(2,1)}, bf16[1536,1408]{1,0:T(8,128)(2,1)}) fusion(f32[1536,2816]{1,0:T(8,128)} %fusion.36, bf16[1408,2048]{1,0:T(8,128)(2,1)} %all-gather.11.cloned.1.call-done, bf16[384,2048]{1,0:T(8,128)(2,1)} %collective-permute-done.15, ...), kind=kOutput, calls=%fused_computation.6 | convolution fusion | flops 8913813504 | bytes 42336256 | tf_op jit(solution)/shard_map/dot_general | solution.py:21
  425.8 15.0 %fusion.3 = bf16[768,2048]{1,0:T(8,128)(2,1)} fusion(bf16[2048,2816]{1,0:T(8,128)(2,1)} %all-gather.9.cloned.1.call-done, bf16[1536,1408]{1,0:T(8,128)(2,1)} %get-tuple-element.26, bf16[1536,1408]{1,0:T(8,128)(2,1)} %get-tuple-element.25), kind=kOutput, calls=%fused_computation.19 | convolution fusion | flops 8868593664 | bytes 23330816 | tf_op jit(solution)/shard_map/dot_general | solution.py:21
  440.9 13.2 %convolution_convert_fusion.1 = bf16[1408,2048]{1,0:T(8,128)(2,1)} fusion(bf16[1536,1408]{1,0:T(8,128)(2,1)S(1)} %copy-done.45, bf16[384,2048]{1,0:T(8,128)(2,1)} %collective-permute-done.15, bf16[384,2048]{1,0:T(8,128)(2,1)} %collective-permute-done.14, bf16[384,2048]{1,0:T(8,128)(2,1)} %collective-permute-done.13, bf16[384,2048]{1,0:T(8,128)(2,1)} %fusion.7), kind=kOutput, calls=%fused_computation.11 | convolution fusion | flops 8886419456 | bytes 16384000 | tf_op jit(solution)/shard_map/dot_general | solution.py:21
  454.1 9.4 convolution_convert_fusion.5
  464.0 1.6 copy-done.17
  465.6 10.8 %add_convert_fusion.1 = bf16[384,2048]{1,0:T(8,128)(2,1)} fusion(bf16[768,2048]{1,0:T(8,128)(2,1)S(1)} %collective-permute-done.16, bf16[2048,2816]{1,0:T(8,128)(2,1)} %all-gather.9.cloned.1.call-done, bf16[1536,1408]{1,0:T(8,128)(2,1)} %get-tuple-element.26, bf16[1536,1408]{1,0:T(8,128)(2,1)} %get-tuple-element.25), kind=kOutput, calls=%fused_computation.41 | convolution fusion | flops 4435869696 | bytes 23330816 | tf_op jit(solution)/shard_map/dot_general | solution.py:21
  477.9 7.3 fusion.33
  485.2 8.1 add_convert_fusion.2
  494.0 19.9 %collective-permute-done.17 = bf16[384,2048]{1,0:T(8,128)(2,1)S(1)} collective-permute-done((bf16[384,2048]{1,0:T(8,128)(2,1)}, bf16[384,2048]{1,0:T(8,128)(2,1)S(1)}, u32[]{:S(2)}, u32[]{:S(2)}) %collective-permute-start.17) | collective-permute-done | bytes 1572896 | tf_op jit(solution)/shard_map/ppermute | solution.py:202
  513.9 12.4 %multiply_reduce_fusion = (f32[384]{0:T(512)S(1)}, f32[384,2048]{1,0:T(8,128)}) fusion(f32[384,2048]{1,0:T(8,128)S(1)} %copy-done.1, f32[384]{0:T(512)S(1)} %copy-done.27, bf16[384,2048]{1,0:T(8,128)(2,1)S(1)} %collective-permute-done.17, bf16[768,2048]{1,0:T(8,128)(2,1)} %copy-done.17, bf16[2048,2816]{1,0:T(8,128)(2,1)} %all-gather.9.cloned.1.call-done, ...), kind=kOutput, calls=%fused_computation.39 | convolution fusion | flops 4439014912 | bytes 29625344 | tf_op jit(solution)/shard_map/dot_general | solution.py:21
  526.3 20.5 %collective-permute-done.12 = bf16[384,2048]{1,0:T(8,128)(2,1)} collective-permute-done((bf16[384,2048]{1,0:T(8,128)(2,1)}, bf16[384,2048]{1,0:T(8,128)(2,1)}, u32[]{:S(2)}, u32[]{:S(2)}) %collective-permute-start.12) | collective-permute-done | bytes 1572896 | tf_op jit(solution)/shard_map/ppermute | solution.py:202
  546.8 7.3 fusion.71
  554.1 1.5 collective-permute-start.18
  555.7 34.0 %collective-permute-done.18 = bf16[384,2048]{1,0:T(8,128)(2,1)S(1)} collective-permute-done((bf16[384,2048]{1,0:T(8,128)(2,1)S(1)}, bf16[384,2048]{1,0:T(8,128)(2,1)S(1)}, u32[]{:S(2)}, u32[]{:S(2)}) %collective-permute-start.18) | collective-permute-done | bytes 1572896 | tf_op jit(solution)/shard_map/ppermute | solution.py:202
  589.7 3.4 collective-permute-done.20
  594.2 4.7 convolution_convert_fusion.6
  599.0 7.5 convolution_convert_fusion.7.refs_0_
  606.5 32.1 %attend_back.1 = bf16[1536,1024]{1,0:T(8,128)(2,1)} custom-call(bf16[1536,512]{1,0:T(8,128)(2,1)} %convolution_convert_fusion.7.refs_0_, bf16[1536,512]{1,0:T(8,128)(2,1)} %get-tuple-element.16.refs_1_, bf16[1536,256]{1,0:T(8,128)(2,1)} %get-tuple-element.17.refs_2_, bf16[1536,256]{1,0:T(8,128)(2,1)} %get-tuple-element.18.refs_3_, ...), custom_call_target="tpu_custom_call" | custom-call | tf_op jit(solution)/shard_map/attend_back/pallas_call | solution.py:172
  638.5 11.2 %convolution_convert_fusion.2 = bf16[2048,1024]{1,0:T(8,128)(2,1)} fusion(bf16[1536,1024]{1,0:T(8,128)(2,1)} %attend_back.1, bf16[384,2048]{1,0:T(8,128)(2,1)} %collective-permute-done.2, bf16[384,2048]{1,0:T(8,128)(2,1)} %collective-permute-done.1, bf16[384,2048]{1,0:T(8,128)(2,1)} %collective-permute-done, bf16[384,2048]{1,0:T(8,128)(2,1)} %fusion.10), kind=kOutput, calls=%fused_computation.18 | convolution fusion | flops 6469713920 | bytes 13631488 | tf_op jit(solution)/shard_map/dot_general | solution.py:21
  651.9 24.5 %convolution_convert_fusion = bf16[2048,2816]{1,0:T(8,128)(2,1)} fusion(bf16[1536,1408]{1,0:T(8,128)(2,1)} %get-tuple-element.25, bf16[1536,1408]{1,0:T(8,128)(2,1)} %get-tuple-element.26, bf16[384,2048]{1,0:T(8,128)(2,1)} %collective-permute-done.10, bf16[384,2048]{1,0:T(8,128)(2,1)S(1)} %copy-done.40, bf16[384,2048]{1,0:T(8,128)(2,1)} %collective-permute-done.8, ...), kind=kOutput, calls=%fused_computation | convolution fusion | flops 17764974592 | bytes 26476544 | tf_op jit(solution)/shard_map/dot_general | solution.py:21
  676.4 1.9 copy-done.8
  678.3 6.0 convolution_convert_fusion.4
  684.5 5.5 collective-permute-done.21
  690.0 3.1 add_convert_fusion
  694.5 2.4 convert_element_type.256
  696.9 1.8 convert_element_type.252
  698.7 58.0 %reduce-scatter.5.cloned.1.call-done = bf16[256,1024]{1,0:T(8,128)(2,1)} async-done(((bf16[2048,1024]{1,0:T(8,128)(2,1)}), bf16[256,1024]{1,0:T(8,128)(2,1)}) %reduce-scatter.5.cloned.1.call-update) | async-done | bytes 524304 | tf_op jit(solution)/shard_map/reduce_scatter | solution.py:227
  756.7 3.5 all-to-all-start.2
  760.2 7.3 fusion.11
  768.9 183.8 %reduce-scatter.9.cloned.1.call-done = bf16[256,2816]{1,0:T(8,128)(2,1)} async-done(((bf16[2048,2816]{1,0:T(8,128)(2,1)}), bf16[256,2816]{1,0:T(8,128)(2,1)}) %reduce-scatter.9.cloned.1.call-update) | async-done | bytes 1441808 | tf_op jit(solution)/shard_map/reduce_scatter | solution.py:227
  952.8 4.0 all-to-all-start.3
  956.7 6.9 fusion.14
  963.9 1.6 copy.71
  965.6 2.0 reshape.174
  970.1 5.2 all-to-all-done.3
  978.1 2.7 copy.69
  980.8 4.0 reshape.178
  986.2 2.7 copy.70
  988.9 3.4 reshape.176
  992.3 3.4 fusion.26
  (188 shorter events, 35.0 us)
Async XLA Ops:
  7.2 97.8 %all-gather.5.cloned.1.call-start = ((), (), s32[]{:S(2)}) async-start(), calls=%async_computation.8 | async-start | bytes 4718592 | tf_op jit(solution)/shard_map/all_gather | solution.py:223
  7.9 15.2 %copy-start.32 = (f32[64]{0:T(128)}, f32[64]{0:T(128)S(1)}, u32[]{:S(2)}) copy-start(f32[64]{0:T(128)S(1)} %convert_element_type.202) | copy-start | bytes 772
  9.0 15.0 %copy-start.44 = (bf16[64]{0:T(256)(128)(2,1)S(1)}, bf16[64]{0:T(256)(128)(2,1)}, u32[]{:S(2)}) copy-start(bf16[64]{0:T(256)(128)(2,1)} %param.24) | copy-start | bytes 388
  9.0 15.0 %copy-start.9 = (bf16[64,5632]{1,0:T(8,128)(2,1)S(1)}, bf16[64,5632]{1,0:T(8,128)(2,1)}, u32[]{:S(2)}) copy-start(bf16[64,5632]{1,0:T(8,128)(2,1)} %param.20) | copy-start | bytes 2162692
  9.0 15.0 %copy-start.10 = (bf16[64,5632]{1,0:T(8,128)(2,1)S(1)}, bf16[64,5632]{1,0:T(8,128)(2,1)}, u32[]{:S(2)}) copy-start(bf16[64,5632]{1,0:T(8,128)(2,1)} %param.21) | copy-start | bytes 2162692
  23.1 123.5 %all-gather.7.cloned.1.call-start = ((), (), s32[]{:S(2)}) async-start(), calls=%async_computation.9 | async-start | bytes 2359296 | tf_op jit(solution)/shard_map/all_gather | solution.py:223
  23.9 286.8 %all-gather.9.cloned.1.call-start = ((), (), s32[]{:S(2)}) async-start(), calls=%async_computation.10 | async-start | bytes 12976128 | tf_op jit(solution)/shard_map/all_gather | solution.py:223
  31.3 22.5 %copy-start.2 = (bf16[2,192,2048]{2,1,0:T(8,128)(2,1)S(1)}, bf16[2,192,2048]{2,1,0:T(8,128)(2,1)}, u32[]{:S(2)}) copy-start(bf16[2,192,2048]{2,1,0:T(8,128)(2,1)} %param.13) | copy-start | bytes 4718596
  53.4 38.5 %copy-start.36 = (s32[2,192]{1,0:T(2,128)S(1)}, s32[2,192]{1,0:T(2,128)}, u32[]{:S(2)}) copy-start(s32[2,192]{1,0:T(2,128)} %param.14) | copy-start | bytes 4612
  53.4 349.9 %all-gather.11.cloned.1.call-start = ((), (), s32[]{:S(2)}) async-start(), calls=%async_computation.11 | async-start | bytes 6488064 | tf_op jit(solution)/shard_map/all_gather | solution.py:223
  54.3 41.3 %copy-start.28 = (f32[384]{0:T(512)}, f32[384]{0:T(512)S(1)}, u32[]{:S(2)}) copy-start(f32[384]{0:T(512)S(1)} %rsqrt.20) | copy-start | bytes 4612
  55.8 36.1 %collective-permute-start = (bf16[384,2048]{1,0:T(8,128)(2,1)}, bf16[384,2048]{1,0:T(8,128)(2,1)}, u32[]{:S(2)}, u32[]{:S(2)}) collective-permute-start(bf16[384,2048]{1,0:T(8,128)(2,1)} %fusion.10), channel_id=1, source_target_pairs={{0,2},{2,0},{1,3},{3,1},{4,6},{6,4},{5,7},{7,5},{8,10},{10,8},{9,1... | collective-permute-start | bytes 4718600 | tf_op jit(solution)/shard_map/ppermute | solution.py:202
  56.2 48.7 %collective-permute-start.1 = (bf16[384,2048]{1,0:T(8,128)(2,1)}, bf16[384,2048]{1,0:T(8,128)(2,1)}, u32[]{:S(2)}, u32[]{:S(2)}) collective-permute-start(bf16[384,2048]{1,0:T(8,128)(2,1)} %fusion.10), channel_id=1, source_target_pairs={{0,1},{1,0},{2,3},{3,2},{4,5},{5,4},{6,7},{7,6},{8,9},{9,8},{10,11... | collective-permute-start | bytes 4718600 | tf_op jit(solution)/shard_map/ppermute | solution.py:202
  91.9 13.0 %collective-permute-start.2 = (bf16[384,2048]{1,0:T(8,128)(2,1)}, bf16[384,2048]{1,0:T(8,128)(2,1)}, u32[]{:S(2)}, u32[]{:S(2)}) collective-permute-start(bf16[384,2048]{1,0:T(8,128)(2,1)} %collective-permute-done), channel_id=1, source_target_pairs={{0,1},{1,0},{2,3},{3,2},{4,5},{5,4},{6,7},{7,6},{8,9},{9,8},{10,11... | collective-permute-start | bytes 4718600 | tf_op jit(solution)/shard_map/ppermute | solution.py:202
  91.9 3.6 collective-permute-start.3
  92.7 3.0 collective-permute-start.4
  95.5 1.2 collective-permute-start.5
  146.6 11.4 %copy-start.20 = (bf16[1536,512]{1,0:T(8,128)(2,1)S(1)}, bf16[1536,512]{1,0:T(8,128)(2,1)}, u32[]{:S(2)}) copy-start(bf16[1536,512]{1,0:T(8,128)(2,1)} %get-tuple-element.15) | copy-start | bytes 4718596
  152.1 6.0 collective-permute-start.6
  152.1 542.5 %reduce-scatter.11.cloned.1.call-start = ((), (), s32[]{:S(2)}) async-start(), calls=%async_computation.15 | async-start | bytes 6488064 | tf_op jit(solution)/shard_map/reduce_scatter | solution.py:227
  152.1 10.7 %copy-start.11 = (bf16[512,2048]{1,0:T(8,128)(2,1)S(1)}, bf16[512,2048]{1,0:T(8,128)(2,1)}, u32[]{:S(2)}) copy-start(bf16[512,2048]{1,0:T(8,128)(2,1)} %all-gather.7.cloned.1.call-done) | copy-start | bytes 6291460
  161.1 36.6 %collective-permute-start.7 = (bf16[384,2048]{1,0:T(8,128)(2,1)S(1)}, bf16[384,2048]{1,0:T(8,128)(2,1)S(1)}, u32[]{:S(2)}, u32[]{:S(2)}) collective-permute-start(bf16[384,2048]{1,0:T(8,128)(2,1)S(1)} %add_convert_fusion.3), channel_id=1, source_target_pairs={{0,2},{2,0},{1,3},{3,1},{4,6},{6,4},{5,7},{7,5},{8,10},{10,8},{9,1... | collective-permute-start | bytes 4718600 | tf_op jit(solution)/shard_map/ppermute | solution.py:202
  202.0 146.7 %copy-start.14 = (bf16[384,2048]{1,0:T(8,128)(2,1)}, bf16[384,2048]{1,0:T(8,128)(2,1)S(1)}, u32[]{:S(2)}) copy-start(bf16[384,2048]{1,0:T(8,128)(2,1)S(1)} %multiply_convert_fusion.4) | copy-start | bytes 4718596
  202.0 37.4 %collective-permute-start.8 = (bf16[384,2048]{1,0:T(8,128)(2,1)S(1)}, bf16[384,2048]{1,0:T(8,128)(2,1)}, u32[]{:S(2)}, u32[]{:S(2)}) collective-permute-start(bf16[384,2048]{1,0:T(8,128)(2,1)S(1)} %multiply_convert_fusion.4), channel_id=1, source_target_pairs={{0,2},{2,0},{1,3},{3,1},{4,6},{6,4},{5,7},{7,5},{8,10},{10,8},{9,1... | collective-permute-start | bytes 4718600 | tf_op jit(solution)/shard_map/ppermute | solution.py:202
  203.8 144.9 %copy-start.30 = (f32[384]{0:T(512)}, f32[384]{0:T(512)S(1)}, u32[]{:S(2)}) copy-start(f32[384]{0:T(512)S(1)} %reshape.180) | copy-start | bytes 4612
  205.3 66.4 %collective-permute-start.13 = (bf16[384,2048]{1,0:T(8,128)(2,1)}, bf16[384,2048]{1,0:T(8,128)(2,1)}, u32[]{:S(2)}, u32[]{:S(2)}) collective-permute-start(bf16[384,2048]{1,0:T(8,128)(2,1)} %fusion.7), channel_id=1, source_target_pairs={{0,2},{2,0},{1,3},{3,1},{4,6},{6,4},{5,7},{7,5},{8,10},{10,8},{9,1... | collective-permute-start | bytes 4718600 | tf_op jit(solution)/shard_map/ppermute | solution.py:202
  205.7 65.9 %collective-permute-start.9 = (bf16[384,2048]{1,0:T(8,128)(2,1)S(1)}, bf16[384,2048]{1,0:T(8,128)(2,1)S(1)}, u32[]{:S(2)}, u32[]{:S(2)}) collective-permute-start(bf16[384,2048]{1,0:T(8,128)(2,1)S(1)} %multiply_convert_fusion.4), channel_id=1, source_target_pairs={{0,1},{1,0},{2,3},{3,2},{4,5},{5,4},{6,7},{7,6},{8,9},{9,8},{10,11... | collective-permute-start | bytes 4718600 | tf_op jit(solution)/shard_map/ppermute | solution.py:202
  239.4 32.2 %collective-permute-start.10 = (bf16[384,2048]{1,0:T(8,128)(2,1)}, bf16[384,2048]{1,0:T(8,128)(2,1)}, u32[]{:S(2)}, u32[]{:S(2)}) collective-permute-start(bf16[384,2048]{1,0:T(8,128)(2,1)} %collective-permute-done.8), channel_id=1, source_target_pairs={{0,1},{1,0},{2,3},{3,2},{4,5},{5,4},{6,7},{7,6},{8,9},{9,8},{10,11... | collective-permute-start | bytes 4718600 | tf_op jit(solution)/shard_map/ppermute | solution.py:202
  239.4 109.3 %collective-permute-start.14 = (bf16[384,2048]{1,0:T(8,128)(2,1)}, bf16[384,2048]{1,0:T(8,128)(2,1)}, u32[]{:S(2)}, u32[]{:S(2)}) collective-permute-start(bf16[384,2048]{1,0:T(8,128)(2,1)} %fusion.7), channel_id=1, source_target_pairs={{0,1},{1,0},{2,3},{3,2},{4,5},{5,4},{6,7},{7,6},{8,9},{9,8},{10,11... | collective-permute-start | bytes 4718600 | tf_op jit(solution)/shard_map/ppermute | solution.py:202
  271.6 77.1 %collective-permute-start.15 = (bf16[384,2048]{1,0:T(8,128)(2,1)}, bf16[384,2048]{1,0:T(8,128)(2,1)}, u32[]{:S(2)}, u32[]{:S(2)}) collective-permute-start(bf16[384,2048]{1,0:T(8,128)(2,1)} %collective-permute-done.13), channel_id=1, source_target_pairs={{0,1},{1,0},{2,3},{3,2},{4,5},{5,4},{6,7},{7,6},{8,9},{9,8},{10,11... | collective-permute-start | bytes 4718600 | tf_op jit(solution)/shard_map/ppermute | solution.py:202
  271.6 77.1 %copy-start.39 = (bf16[384,2048]{1,0:T(8,128)(2,1)}, bf16[384,2048]{1,0:T(8,128)(2,1)S(1)}, u32[]{:S(2)}) copy-start(bf16[384,2048]{1,0:T(8,128)(2,1)S(1)} %collective-permute-done.9) | copy-start | bytes 4718596
  425.8 15.0 %copy-start.45 = (bf16[1536,1408]{1,0:T(8,128)(2,1)S(1)}, bf16[1536,1408]{1,0:T(8,128)(2,1)}, u32[]{:S(2)}) copy-start(bf16[1536,1408]{1,0:T(8,128)(2,1)} %get-tuple-element.27) | copy-start | bytes 12976132
  440.8 23.2 %collective-permute-start.16 = (bf16[768,2048]{1,0:T(8,128)(2,1)}, bf16[768,2048]{1,0:T(8,128)(2,1)S(1)}, u32[]{:S(2)}, u32[]{:S(2)}) collective-permute-start(bf16[768,2048]{1,0:T(8,128)(2,1)} %fusion.3), channel_id=1, source_target_pairs={{0,1},{1,0},{2,3},{3,2},{4,5},{5,4},{6,7},{7,6},{8,9},{9,8},{10,11... | collective-permute-start | bytes 9437192 | tf_op jit(solution)/shard_map/ppermute | solution.py:202
  454.1 242.9 %reduce-scatter.7.cloned.1.call-start = ((), (), s32[]{:S(2)}) async-start(), calls=%async_computation.13 | async-start | bytes 2359296 | tf_op jit(solution)/shard_map/reduce_scatter | solution.py:227
  463.5 21.7 %collective-permute-start.11 = (bf16[768,2048]{1,0:T(8,128)(2,1)}, bf16[768,2048]{1,0:T(8,128)(2,1)S(1)}, u32[]{:S(2)}, u32[]{:S(2)}) collective-permute-start(bf16[768,2048]{1,0:T(8,128)(2,1)} %convolution_convert_fusion.5), channel_id=1, source_target_pairs={{0,1},{1,0},{2,3},{3,2},{4,5},{5,4},{6,7},{7,6},{8,9},{9,8},{10,11... | collective-permute-start | bytes 9437192 | tf_op jit(solution)/shard_map/ppermute | solution.py:202
  476.4 37.5 %collective-permute-start.17 = (bf16[384,2048]{1,0:T(8,128)(2,1)}, bf16[384,2048]{1,0:T(8,128)(2,1)S(1)}, u32[]{:S(2)}, u32[]{:S(2)}) collective-permute-start(bf16[384,2048]{1,0:T(8,128)(2,1)} %add_convert_fusion.1), channel_id=1, source_target_pairs={{0,2},{2,0},{1,3},{3,1},{4,6},{6,4},{5,7},{7,5},{8,10},{10,8},{9,1... | collective-permute-start | bytes 4718600 | tf_op jit(solution)/shard_map/ppermute | solution.py:202
  485.2 28.7 %copy-start.1 = (f32[384,2048]{1,0:T(8,128)S(1)}, f32[384,2048]{1,0:T(8,128)}, u32[]{:S(2)}) copy-start(f32[384,2048]{1,0:T(8,128)} %copy-done) | copy-start | bytes 9437188
  485.2 28.7 %copy-start.27 = (f32[384]{0:T(512)S(1)}, f32[384]{0:T(512)}, u32[]{:S(2)}) copy-start(f32[384]{0:T(512)} %copy-done.26) | copy-start | bytes 4612
  485.2 8.1 copy-start.18
  493.3 53.5 %copy-start.5 = (bf16[2,192,2048]{2,1,0:T(8,128)(2,1)S(1)}, bf16[2,192,2048]{2,1,0:T(8,128)(2,1)}, u32[]{:S(2)}) copy-start(bf16[2,192,2048]{2,1,0:T(8,128)(2,1)} %param.25) | copy-start | bytes 4718596
  493.3 53.5 %copy-start.31 = (f32[384]{0:T(512)S(1)}, f32[384]{0:T(512)}, u32[]{:S(2)}) copy-start(f32[384]{0:T(512)} %copy-done.30) | copy-start | bytes 4612
  493.3 53.4 %collective-permute-start.12 = (bf16[384,2048]{1,0:T(8,128)(2,1)}, bf16[384,2048]{1,0:T(8,128)(2,1)}, u32[]{:S(2)}, u32[]{:S(2)}) collective-permute-start(bf16[384,2048]{1,0:T(8,128)(2,1)} %add_convert_fusion.2), channel_id=1, source_target_pairs={{0,2},{2,0},{1,3},{3,1},{4,6},{6,4},{5,7},{7,5},{8,10},{10,8},{9,1... | collective-permute-start | bytes 4718600 | tf_op jit(solution)/shard_map/ppermute | solution.py:202
  546.8 47.4 %copy-start.21 = (bf16[1536,512]{1,0:T(8,128)(2,1)S(1)}, bf16[1536,512]{1,0:T(8,128)(2,1)}, u32[]{:S(2)}) copy-start(bf16[1536,512]{1,0:T(8,128)(2,1)} %get-tuple-element.15) | copy-start | bytes 4718596
  554.1 39.0 %copy-start.13 = (bf16[384,2048]{1,0:T(8,128)(2,1)}, bf16[384,2048]{1,0:T(8,128)(2,1)S(1)}, u32[]{:S(2)}) copy-start(bf16[384,2048]{1,0:T(8,128)(2,1)S(1)} %get-tuple-element.21) | copy-start | bytes 4718596
  554.1 44.8 %copy-start.12 = (bf16[512,2048]{1,0:T(8,128)(2,1)S(1)}, bf16[512,2048]{1,0:T(8,128)(2,1)}, u32[]{:S(2)}) copy-start(bf16[512,2048]{1,0:T(8,128)(2,1)} %all-gather.7.cloned.1.call-done) | copy-start | bytes 6291460
  554.1 35.5 %collective-permute-start.18 = (bf16[384,2048]{1,0:T(8,128)(2,1)S(1)}, bf16[384,2048]{1,0:T(8,128)(2,1)S(1)}, u32[]{:S(2)}, u32[]{:S(2)}) collective-permute-start(bf16[384,2048]{1,0:T(8,128)(2,1)S(1)} %get-tuple-element.21), channel_id=1, source_target_pairs={{0,2},{2,0},{1,3},{3,1},{4,6},{6,4},{5,7},{7,5},{8,10},{10,8},{9,1... | collective-permute-start | bytes 4718600 | tf_op jit(solution)/shard_map/ppermute | solution.py:202
  555.6 34.0 %collective-permute-start.19 = (bf16[384,2048]{1,0:T(8,128)(2,1)S(1)}, bf16[384,2048]{1,0:T(8,128)(2,1)S(1)}, u32[]{:S(2)}, u32[]{:S(2)}) collective-permute-start(bf16[384,2048]{1,0:T(8,128)(2,1)S(1)} %get-tuple-element.21), channel_id=1, source_target_pairs={{0,1},{1,0},{2,3},{3,2},{4,5},{5,4},{6,7},{7,6},{8,9},{9,8},{10,11... | collective-permute-start | bytes 4718600 | tf_op jit(solution)/shard_map/ppermute | solution.py:202
  589.7 3.4 collective-permute-start.20
  598.9 157.8 %reduce-scatter.5.cloned.1.call-start = ((), (), s32[]{:S(2)}) async-start(), calls=%async_computation.12 | async-start | bytes 4718592 | tf_op jit(solution)/shard_map/reduce_scatter | solution.py:227
  649.8 303.0 %reduce-scatter.9.cloned.1.call-start = ((), (), s32[]{:S(2)}) async-start(), calls=%async_computation.14 | async-start | bytes 12976128 | tf_op jit(solution)/shard_map/reduce_scatter | solution.py:227
  678.3 11.7 %copy-start.38 = (bf16[2048,1024]{1,0:T(8,128)(2,1)S(1)}, bf16[2048,1024]{1,0:T(8,128)(2,1)}, u32[]{:S(2)}) copy-start(bf16[2048,1024]{1,0:T(8,128)(2,1)} %all-gather.5.cloned.1.call-done) | copy-start | bytes 12582916
  684.3 5.7 collective-permute-start.21
  693.1 67.1 %copy-start.3 = (bf16[2,192,2048]{2,1,0:T(8,128)(2,1)S(1)}, bf16[2,192,2048]{2,1,0:T(8,128)(2,1)}, u32[]{:S(2)}) copy-start(bf16[2,192,2048]{2,1,0:T(8,128)(2,1)} %param.13) | copy-start | bytes 4718596
  693.1 67.1 %copy-start.29 = (f32[384]{0:T(512)S(1)}, f32[384]{0:T(512)}, u32[]{:S(2)}) copy-start(f32[384]{0:T(512)} %copy-done.28) | copy-start | bytes 4612
  693.1 67.1 %collective-permute-start.22 = (bf16[384,2048]{1,0:T(8,128)(2,1)}, bf16[384,2048]{1,0:T(8,128)(2,1)}, u32[]{:S(2)}, u32[]{:S(2)}) collective-permute-start(bf16[384,2048]{1,0:T(8,128)(2,1)} %add_convert_fusion), channel_id=1, source_target_pairs={{0,2},{2,0},{1,3},{3,1},{4,6},{6,4},{5,7},{7,5},{8,10},{10,8},{9,1... | collective-permute-start | bytes 4718600 | tf_op jit(solution)/shard_map/ppermute | solution.py:202
  756.7 12.3 %all-to-all-start.2 = ((bf16[4,64,1024]{2,1,0:T(8,128)(2,1)}), bf16[4,64,1024]{2,1,0:T(8,128)(2,1)S(1)}, u32[]{:S(2)}, u32[]{:S(2)}) async-start(bf16[4,64,1024]{2,1,0:T(8,128)(2,1)} %bitcast.86), calls=%async_computation.3 | async-start | bytes 1048576 | tf_op jit(solution)/shard_map/all_to_all | solution.py:231
  952.8 22.6 %all-to-all-start.3 = ((bf16[4,64,2816]{2,1,0:T(8,128)(2,1)}), bf16[4,64,2816]{2,1,0:T(8,128)(2,1)S(1)}, u32[]{:S(2)}, u32[]{:S(2)}) async-start(bf16[4,64,2816]{2,1,0:T(8,128)(2,1)} %bitcast.85), calls=%async_computation.6 | async-start | bytes 2883584 | tf_op jit(solution)/shard_map/all_to_all | solution.py:231
  963.9 3.9 copy-start.23
  963.9 3.9 copy-start.25
  963.9 3.9 copy-start.33
  963.9 4.7 copy-start.16
  978.1 6.7 copy-start.6
  986.2 6.1 copy-start.7
  986.2 6.1 copy-start.35
  (15 other events, 35.0 us)
Sparse Core Ops, SparseCore 0:
  23.2 73.5 all-gather.4
  99.0 47.6 all-gather.6
  148.8 161.8 all-gather.8
  312.8 90.4 all-gather.10
  454.2 108.9 reduce-scatter.10
  599.0 66.5 reduce-scatter.6
  669.3 87.3 reduce-scatter.4
  760.3 192.4 reduce-scatter.8

commit v2 on v1

--- a/solution.py
+++ b/solution.py
@@ -219,28 +219,71 @@
     return own + from_chip.astype(F32)
 
 
-def gather_rows(value):
-    return lax.all_gather(value, ("dp", "y"), axis=0, tiled=True)
-
-
-def scatter_rows(value):
-    return lax.psum_scatter(value, ("dp", "y"), scatter_dimension=0, tiled=True)
+def gather_z(value):
+    return lax.all_gather(value, "dp", axis=0, tiled=True)
+
+
+def scatter_z(value):
+    return lax.psum_scatter(value, "dp", scatter_dimension=0, tiled=True)
 
 
 def exchange(value):
     return lax.all_to_all(value, ("x", "c"), 0, 0, tiled=True)
 
 
-def by_rank(weight, piece):
+def in_y_order(own, other):
+    first = lax.axis_index("y") == 0
+    return jnp.where(first, own, other), jnp.where(first, other, own)
+
+
+def own_columns(value, block):
+    parts = [value[:, at : at + block] for at in range(0, value.shape[1], block)]
+    return in_y_order(jnp.concatenate(parts[::2], axis=1), jnp.concatenate(parts[1::2], axis=1))
+
+
+def whole_columns(own, other, block):
+    zero, one = in_y_order(own, other)
+    parts = []
+    for at in range(0, own.shape[1], block):
+        parts += [zero[:, at : at + block], one[:, at : at + block]]
+    return jnp.concatenate(parts, axis=1)
+
+
+def gather_pair(value):
+    own = gather_z(value)
+    return own, swap(own, "y")
+
+
+def scatter_pair(own, other, right):
+    sent = swap(inner_rows(other, right).astype(BF16), "y")
+    return scatter_z((inner_rows(own, right) + sent.astype(F32)).astype(BF16))
+
+
+def heads_by_rank(weight):
     rows, columns = weight.shape
-    parts = weight.reshape(rows, columns // (RANKS * piece), RANKS, piece)
+    parts = weight.reshape(rows, columns // (RANKS * HEAD_DIM), RANKS, HEAD_DIM)
     return parts.transpose(2, 0, 1, 3).reshape(RANKS * rows, columns // RANKS)
 
 
-def from_ranks(value, piece):
+def heads_from_ranks(value):
     ranks, rows, columns = value.shape
-    parts = value.reshape(ranks, rows, columns // piece, piece)
+    parts = value.reshape(ranks, rows, columns // HEAD_DIM, HEAD_DIM)
     return parts.transpose(1, 2, 0, 3).reshape(rows, ranks * columns)
+
+
+def units_by_rank(weight, depth, piece, low, high):
+    rows = weight.shape[0]
+    parts = weight.reshape(rows, depth, 2, RANKS, piece)[..., low:high]
+    return parts.transpose(3, 0, 2, 1, 4).reshape(RANKS * rows, 2 * depth * (high - low))
+
+
+def units_from_ranks(pieces, depth):
+    parts = []
+    for value in pieces:
+        ranks, rows, columns = value.shape
+        parts.append(value.reshape(ranks, rows, 2, depth, columns // (2 * depth)))
+    parts = [value.transpose(1, 3, 2, 0, 4) for value in parts]
+    return jnp.concatenate(parts, axis=-1).reshape(rows, -1)
 
 
 def unit(value):
@@ -273,7 +316,11 @@
     piece = w_down.shape[0]
     width = w_query.shape[1] // RANKS
     side = w_key.shape[1]
-    hidden_units = w_gate.shape[1] // RANKS
+    depth = lax.axis_size("dp")
+    block = RANKS * owned
+    half = model // 2
+    cut = -(-piece // 32) * 16
+    chunks = ((0, cut), (cut, piece))
     span = jnp.arange(rows, dtype=jnp.int32)
     valid = (span[None, :] < live_counts).astype(F32).reshape(tokens, 1)
 
@@ -282,60 +329,82 @@
     scaled = lambda weight, gain: (weight.astype(F32) * gain).astype(BF16)
     side_weights = jnp.concatenate([scaled(w_key, gain1), scaled(w_value, gain1)], axis=1)
     qkv_sent = jnp.concatenate(
-        [by_rank(scaled(w_query, gain1), HEAD_DIM), jnp.tile(side_weights, (RANKS, 1))], axis=1
+        [heads_by_rank(scaled(w_query, gain1)), jnp.tile(side_weights, (RANKS, 1))], axis=1
     )
-    gu_sent = jnp.concatenate(
-        [by_rank(scaled(w_gate, gain2), piece), by_rank(scaled(w_up, gain2), piece)], axis=1
-    )
-    w_qkv = gather_rows(exchange(qkv_sent))
-    wo = gather_rows(w_out)
-    w_gu = gather_rows(exchange(gu_sent))
-    wd = gather_rows(w_down)
-
+    w_qkv = gather_pair(exchange(qkv_sent))
+
+    inputs = layer_input.reshape(tokens, model).astype(F32)
+    n1, r1 = unit(inputs)
+    n1_own, n1_other = own_columns(n1.astype(BF16), block)
+    n1_all = gather_group(jnp.concatenate([n1_own, n1_other], axis=1))
     segments = gather_group(segment_ids)
     table = rope_table(segments)
 
-    inputs = layer_input.reshape(tokens, model).astype(F32)
-    n1, r1 = unit(inputs)
-    n1_all = gather_group(n1.astype(BF16))
+    wo = gather_z(jnp.concatenate(in_y_order(w_out, swap(w_out, "y")), axis=0))
+    low_gate, low_up = scaled(w_gate, gain2), scaled(w_up, gain2)
+    w_gu = []
+    for low, high in chunks:
+        sent = [units_by_rank(weight, depth, piece, low, high) for weight in (low_gate, low_up)]
+        w_gu.append(gather_pair(exchange(jnp.concatenate(sent, axis=1))))
+    wd = [
+        jnp.concatenate(in_y_order(*gather_pair(w_down[low:high])), axis=0) for low, high in chunks
+    ]
     error = out_grad.reshape(tokens, model).astype(F32) * valid
     error_all = gather_group(error.astype(BF16))
 
-    qkv = forward_dot(n1_all, w_qkv)
+    qkv = forward_dot(n1_all, jnp.concatenate(w_qkv, axis=0))
     mixed, q_rot, k_rot, values = attend(qkv, table, segments, width, side)
     hidden = inputs + reduce_group(lambda left: forward_dot(left, wo), mixed)
 
     n2, r2 = unit(hidden)
-    n2_all = gather_group(n2.astype(BF16))
-    gate_up = forward_dot(n2_all, w_gu)
-    gate, upward = gate_up[:, :hidden_units], gate_up[:, hidden_units:]
-    sigma = jax.nn.sigmoid(gate)
-    silu_gate = gate * sigma
-    inner = (silu_gate * upward).astype(BF16)
-    result = hidden + reduce_group(lambda left: forward_dot(left, wd), inner)
-    layer_output = (result * valid).astype(BF16).reshape(micro, rows, model)
-
-    grad_wd = scatter_rows(inner_rows(inner, error_all).astype(BF16)).astype(F32)
-    grad_inner = against(error_all, wd)
-    grad_gate = grad_inner * upward * (sigma + gate * sigma * (1.0 - sigma))
-    grad_up = grad_inner * silu_gate
-    grad_gu = jnp.concatenate([grad_gate.astype(BF16), grad_up.astype(BF16)], axis=1)
-    gu_raw = exchange(scatter_rows(inner_rows(n2_all, grad_gu).astype(BF16)))
-    grad_n2 = reduce_group(lambda left: against(left, w_gu), grad_gu)
+    n2_own, n2_other = own_columns(n2.astype(BF16), block)
+    n2_all = gather_group(jnp.concatenate([n2_own, n2_other], axis=1))
+    inners, grad_gus, raw_gus, grad_wds = [], [], [], []
+    for index in range(len(chunks)):
+        gate_up = forward_dot(n2_all, jnp.concatenate(w_gu[index], axis=0))
+        units = gate_up.shape[1] // 2
+        gate, upward = gate_up[:, :units], gate_up[:, units:]
+        sigma = jax.nn.sigmoid(gate)
+        silu_gate = gate * sigma
+        inner = (silu_gate * upward).astype(BF16)
+        own, other = in_y_order(inner[:, : units // 2], inner[:, units // 2 :])
+        grad_wds.append(scatter_pair(own, other, error_all))
+        grad_inner = against(error_all, wd[index])
+        grad_gate = grad_inner * upward * (sigma + gate * sigma * (1.0 - sigma))
+        grad_up = grad_inner * silu_gate
+        grad_gu = jnp.concatenate([grad_gate.astype(BF16), grad_up.astype(BF16)], axis=1)
+        raw = exchange(scatter_pair(n2_all[:, :half], n2_all[:, half:], grad_gu))
+        raw_gus.append(raw.reshape(RANKS, owned, 2 * units).astype(F32))
+        inners.append(inner)
+        grad_gus.append(grad_gu)
+    inner = jnp.concatenate(inners, axis=1)
+    grad_gu = jnp.concatenate(grad_gus, axis=1)
+    wd_all = jnp.concatenate(wd, axis=0)
+    gu_own = jnp.concatenate([weight[0] for weight in w_gu], axis=1)
+    gu_other = jnp.concatenate([weight[1] for weight in w_gu], axis=1)
+    gu_all = jnp.concatenate([gu_own, gu_other], axis=0)
+
+    grad_n2 = reduce_group(lambda left: against(left, gu_all), grad_gu)
+    grad_n2 = whole_columns(grad_n2[:, :half], grad_n2[:, half:], block)
     grad_hidden = error + unit_back(n2, r2, grad_n2)
     hidden_all = gather_group(grad_hidden.astype(BF16))
     grad_mixed = against(hidden_all, wo).astype(BF16)
-    grad_wo = scatter_rows(inner_rows(mixed, hidden_all).astype(BF16)).astype(F32)
+    mixed_own, mixed_other = own_columns(mixed, owned)
+    grad_wo = scatter_pair(mixed_own, mixed_other, hidden_all).astype(F32)
     grad_qkv = attend_back(grad_mixed, q_rot, k_rot, values, table, segments, width, side)
-    qkv_raw = exchange(scatter_rows(inner_rows(n1_all, grad_qkv).astype(BF16)))
-    grad_n1 = reduce_group(lambda left: against(left, w_qkv), grad_qkv)
+    qkv_raw = exchange(scatter_pair(n1_all[:, :half], n1_all[:, half:], grad_qkv))
+    grad_n1 = reduce_group(lambda left: against(left, jnp.concatenate(w_qkv, axis=0)), grad_qkv)
+    grad_n1 = whole_columns(grad_n1[:, :half], grad_n1[:, half:], block)
     input_grad = (grad_hidden + unit_back(n1, r1, grad_n1)).reshape(micro, rows, model)
 
-    gu_raw = gu_raw.reshape(RANKS, owned, 2 * hidden_units).astype(F32)
-    raw_gate = from_ranks(gu_raw[:, :, :hidden_units], piece)
-    raw_up = from_ranks(gu_raw[:, :, hidden_units:], piece)
+    result = hidden + reduce_group(lambda left: forward_dot(left, wd_all), inner)
+    layer_output = (result * valid).astype(BF16).reshape(micro, rows, model)
+
+    halves = [raw.shape[2] // 2 for raw in raw_gus]
+    raw_gate = units_from_ranks([raw[..., :n] for raw, n in zip(raw_gus, halves)], depth)
+    raw_up = units_from_ranks([raw[..., n:] for raw, n in zip(raw_gus, halves)], depth)
     qkv_raw = qkv_raw.reshape(RANKS, owned, width + 2 * side).astype(F32)
-    raw_query = from_ranks(qkv_raw[:, :, :width], HEAD_DIM)
+    raw_query = heads_from_ranks(qkv_raw[:, :, :width])
     raw_side = jnp.sum(qkv_raw[:, :, width:], axis=0)
     raw_key, raw_value = raw_side[:, :side], raw_side[:, side:]
     row_dot = lambda raw, weight: jnp.sum(raw * weight.astype(F32), axis=1)
@@ -350,7 +419,7 @@
         grad_wo,
         raw_gate * gain2,
         raw_up * gain2,
-        grad_wd,
+        jnp.concatenate(grad_wds, axis=0).astype(F32),
         grad_gain1,
         grad_gain2,
     )
@@ -485,7 +554,7 @@
 
     def step(*args):
         whole_heads = args[6].shape[0] == HEAD_DIM * mesh.size
-        body = layer if whole_heads else plain_layer
+        body = layer if whole_heads and inner == 2 * RANKS else plain_layer
         return jax.shard_map(
             body, mesh=grid, in_specs=in_specs, out_specs=out_specs, check_vma=False
         )(*args)

time: 1010 us -> 982 us (0.972)
  waiting for transfers between devices: 576 us -> 415 us
  other arithmetic: 36.6 us -> 76.5 us
  matrix products: 224 us -> 254 us
  local copies, waits for them, and re-layouts: 42.1 us -> 71.9 us
  starting transfers between devices: 19.7 us -> 36.8 us
  blocking collectives: 34.9 us -> 47.2 us
    reduce_scatter x4 -> x6, waiting for transfers between devices: 242 us -> 6.14 us  [scatter_z(): return lax.psum_scatter(value, 'dp', scatter_dimension=0, tiled=True)]
    ppermute x23 -> x35, waiting for transfers between devices: 228 us -> 395 us  [swap(): return lax.ppermute(value, axis, [(0, 1), (1, 0)])]
    all_gather x4 -> x6, waiting for transfers between devices: 98.8 us -> 10.6 us  [gather_z(): return lax.all_gather(value, 'dp', axis=0, tiled=True)]
    dot_general x20 -> x30, matrix products: 224 us -> 254 us  [contract(): lax.dot_general(left, right, (dims, ((), ())), preferred_element_type=F32)]
    concatenate x2 -> x11, other arithmetic: 0.16 us -> 27.4 us  [the longest x2 11.6 us: gather_group(): return jnp.concatenate([value, across, beside, beside_across], axis=0)]
    unnamed x92 -> x174, local copies, waits for them, and re-layouts: 8.67 us -> 22.1 us
    all_to_all x2, blocking collectives: 34.9 us -> 47.2 us  [exchange(): return lax.all_to_all(value, ('x', 'c'), 0, 0, tiled=True)]
    ppermute x23 -> x35, starting transfers between devices: 11.6 us -> 21.5 us  [swap(): return lax.ppermute(value, axis, [(0, 1), (1, 0)])]
  transfers between devices with their start and end apart: 33 -> 51, of which waited for: 20 -> 19; matrix products, arithmetic and copies ran while one was open for 23% -> 34% of each run, Pallas kernels for 5% -> 6%
where the time goes in v2:
time: 982 us; the launch traced here: 973 us
  waiting for transfers between devices  415 us (42%)
  matrix products  254 us (26%)
  other arithmetic  76.5 us (8%)
  local copies, waits for them, and re-layouts  71.9 us (7%)
  Pallas kernels  55.3 us (6%)
  blocking collectives  47.2 us (5%)
  starting transfers between devices  36.8 us (4%)
  between operations  15.8 us (2%)
    ppermute x35, waiting for transfers between devices, swap(): return lax.ppermute(value, axis, [(0, 1), (1, 0)])  395 us
    dot_general x30, matrix products, contract(): lax.dot_general(left, right, (dims, ((), ())), preferred_element_type=F32)  254 us
    all_to_all x2, blocking collectives, exchange(): return lax.all_to_all(value, ('x', 'c'), 0, 0, tiled=True)  47.2 us
    pallas_call x1, Pallas kernels, attend_back(): pl.pallas_call(kernel, grid=(blocks,), in_specs=[rows_spec(rows, width),...  32.2 us
    pallas_call x1, Pallas kernels, attend(): pl.pallas_call(kernel, grid=(blocks,), in_specs=[rows_spec(rows, qkv.shap...  23 us
    unnamed x174, local copies, waits for them, and re-layouts  22.1 us
    ppermute x35, starting transfers between devices, swap(): return lax.ppermute(value, axis, [(0, 1), (1, 0)])  21.5 us
  transfers between devices with their start and end apart: 51, of which 19 were waited for; matrix products, arithmetic and copies ran while one was open for 34% of the time, Pallas kernels for 6%

profile of v2, /device:TPU:0, one launch (start us, length us, event | category | flops | bytes accessed | tf_op | source)
XLA Modules:
  0.0 973.1 jit_solution(12235105779800839853)
XLA Ops:
  10.2 13.0 %all_to_all.54 = bf16[4,64,1024]{2,1,0:T(8,128)(2,1)} all-to-all(bf16[4,64,1024]{2,1,0:T(8,128)(2,1)S(1)} %pad_maximum_fusion.26), channel_id=1, replica_groups=mesh['dp'=4,'y'=2,'x'=2,'c'=2] {'x','c'}, dimensions={0} | all-to-all | bytes 1048576 | tf_op jit(solution)/shard_map/all_to_all | solution.py:231
  32.3 32.4 %collective-permute-done = bf16[384,2048]{1,0:T(8,128)(2,1)} collective-permute-done((bf16[384,2048]{1,0:T(8,128)(2,1)}, bf16[384,2048]{1,0:T(8,128)(2,1)}, u32[]{:S(2)}, u32[]{:S(2)}) %collective-permute-start) | collective-permute-done | bytes 1572896 | tf_op jit(solution)/shard_map/ppermute | solution.py:202
  67.0 4.3 reshape.209
  80.6 3.5 all-to-all-start.1
  86.4 9.3 collective-permute-done.4
  106.6 4.2 pad_maximum_fusion.1
  111.0 23.4 %collective-permute-done.3 = bf16[1024,1024]{1,0:T(8,128)(2,1)} collective-permute-done((bf16[1024,1024]{1,0:T(8,128)(2,1)}, bf16[1024,1024]{1,0:T(8,128)(2,1)}, u32[]{:S(2)}, u32[]{:S(2)}) %collective-permute-start.3) | collective-permute-done | bytes 2097184 | tf_op jit(solution)/shard_map/ppermute | solution.py:202
  138.2 8.5 fusion.129.refs_0_
  146.7 23.0 %attend.1 = (bf16[1536,512]{1,0:T(8,128)(2,1)}, bf16[1536,512]{1,0:T(8,128)(2,1)}, bf16[1536,256]{1,0:T(8,128)(2,1)}, bf16[1536,256]{1,0:T(8,128)(2,1)}) custom-call(f32[1536,1024]{1,0:T(8,128)} %fusion.129.refs_0_, f32[1536,256]{1,0:T(8,128)} %concatenate.157.refs_1_.refs_4_, s32[8,192,1]{2,1,0:T(8,128)} %copy.57.refs_2_.refs_5_, ...), custom_call_target="tpu_custom_call" | custom-call | tf_op jit(solution)/shard_map/attend/pallas_call | solution.py:148
  169.8 5.4 convolution_convert_fusion.2
  181.2 4.2 add_convert_fusion.7
  194.8 34.3 %all_to_all.55 = bf16[4,64,1280]{2,1,0:T(8,128)(2,1)} all-to-all(bf16[4,64,1280]{2,1,0:T(8,128)(2,1)S(1)} %pad_maximum_fusion.25), channel_id=1, replica_groups=mesh['dp'=4,'y'=2,'x'=2,'c'=2] {'x','c'}, dimensions={0} | all-to-all | bytes 1310720 | tf_op jit(solution)/shard_map/all_to_all | solution.py:231
  240.5 10.6 %all-gather.15.cloned.1.call-done = bf16[384,2048]{1,0:T(8,128)(2,1)} async-done(((bf16[96,2048]{1,0:T(8,128)(2,1)}), bf16[384,2048]{1,0:T(8,128)(2,1)}) %all-gather.15.cloned.1.call-update) | async-done | bytes 1572880 | tf_op jit(solution)/shard_map/all_gather | solution.py:223
  255.6 73.2 %collective-permute-done.16 = bf16[320,2048]{1,0:T(8,128)(2,1)} collective-permute-done((bf16[320,2048]{1,0:T(8,128)(2,1)}, bf16[320,2048]{1,0:T(8,128)(2,1)}, u32[]{:S(2)}, u32[]{:S(2)}) %collective-permute-start.16) | collective-permute-done | bytes 1310752 | tf_op jit(solution)/shard_map/ppermute | solution.py:202
  329.3 32.0 %collective-permute-done.15 = bf16[384,2048]{1,0:T(8,128)(2,1)} collective-permute-done((bf16[384,2048]{1,0:T(8,128)(2,1)}, bf16[384,2048]{1,0:T(8,128)(2,1)}, u32[]{:S(2)}, u32[]{:S(2)}) %collective-permute-start.15) | collective-permute-done | bytes 1572896 | tf_op jit(solution)/shard_map/ppermute | solution.py:202
  361.6 3.5 broadcast_select_fusion.3
  365.2 3.4 broadcast_select_fusion.1
  369.0 18.2 %fusion = f32[1536,1536]{0,1:T(8,128)} fusion(bf16[1024,1536]{1,0:T(8,128)(2,1)} %collective-permute-done.13, bf16[1024,1536]{1,0:T(8,128)(2,1)} %all-gather.11.cloned.1.call-done, bf16[384,2048]{1,0:T(8,128)(2,1)} %collective-permute-done.12, bf16[384,2048]{1,0:T(8,128)(2,1)S(1)} %collective-permute-done.11, bf16[384,2048]{1,0:T(8,128)(2,1)} %collective-permute-done.10, ...), kind=kOutput, calls=%fused_computation.4 | convolution fusion | flops 9707716608 | bytes 22020096 | tf_op jit(solution)/shard_map/dot_general | solution.py:21
  387.3 32.0 %collective-permute-done.14 = bf16[1024,1280]{1,0:T(8,128)(2,1)} collective-permute-done((bf16[1024,1280]{1,0:T(8,128)(2,1)}, bf16[1024,1280]{1,0:T(8,128)(2,1)}, u32[]{:S(2)}, u32[]{:S(2)}) %collective-permute-start.14) | collective-permute-done | bytes 2621472 | tf_op jit(solution)/shard_map/ppermute | solution.py:202
  419.3 14.9 %fusion.4 = f32[1536,1280]{0,1:T(8,128)} fusion(bf16[1024,1280]{1,0:T(8,128)(2,1)} %collective-permute-done.14, bf16[1024,1280]{1,0:T(8,128)(2,1)} %all-gather.13.cloned.1.call-done, bf16[384,2048]{1,0:T(8,128)(2,1)} %collective-permute-done.12, bf16[384,2048]{1,0:T(8,128)(2,1)S(1)} %collective-permute-done.11, ...), kind=kOutput, calls=%fused_computation.12 | convolution fusion | flops 8095006720 | bytes 19398656 | tf_op jit(solution)/shard_map/dot_general | solution.py:21
  434.3 12.9 %multiply_convert_fusion.4 = (bf16[1536,640]{0,1:T(8,128)(2,1)S(1)}, bf16[1536,640]{0,1:T(8,128)(2,1)}, bf16[1536,640]{0,1:T(8,128)(2,1)}) fusion(f32[1536,1280]{0,1:T(8,128)} %fusion.4, bf16[320,2048]{1,0:T(8,128)(2,1)} %get-tuple-element.39, bf16[320,2048]{1,0:T(8,128)(2,1)} %get-tuple-element.38, bf16[384,2048]{1,0:T(8,128)(2,1)} %collective-permute-done.21, ...), kind=kOutput, calls=%fused_computation.30 | convolution fusion | flops 4070703104 | bytes 22675456 | tf_op jit(solution)/shard_map/dot_general | solution.py:21
  447.2 14.5 %multiply_convert_fusion.1 = (bf16[1536,768]{0,1:T(8,128)(2,1)}, bf16[1536,768]{0,1:T(8,128)(2,1)}, bf16[1536,768]{0,1:T(8,128)(2,1)}) fusion(f32[1536,1536]{0,1:T(8,128)} %fusion, bf16[384,2048]{1,0:T(8,128)(2,1)} %get-tuple-element.37, bf16[384,2048]{1,0:T(8,128)(2,1)S(1)} %copy-done.29, bf16[384,2048]{1,0:T(8,128)(2,1)} %collective-permute-done.21, ...), kind=kOutput, calls=%fused_computation.19 | convolution fusion | flops 4879810560 | bytes 25952256 | tf_op jit(solution)/shard_map/dot_general | solution.py:21
  461.7 6.9 pad_maximum_fusion
  468.6 18.4 %fusion.10 = bf16[768,2048]{1,0:T(8,128)(2,1)} fusion(bf16[1536,2816]{0,1:T(8,128)(2,1)} %pad_maximum_fusion, bf16[1024,1280]{1,0:T(8,128)(2,1)} %collective-permute-done.14, bf16[1024,1536]{1,0:T(8,128)(2,1)} %collective-permute-done.13, bf16[1024,1280]{1,0:T(8,128)(2,1)} %all-gather.13.cloned.1.call-done, bf16[1024,1536]{1,0:T(8,128)(2,1)} %all-gather.11.cloned.1.call-done), kind=kOutput, calls=%fused_computation.38 | convolution fusion | flops 8906080256 | bytes 19005440 | tf_op jit(solution)/shard_map/dot_general | solution.py:21
  487.0 9.1 convolution_convert_fusion.4
  496.6 4.4 convolution_convert_fusion.7
  501.3 7.4 pad_maximum_fusion.2
  508.8 6.2 convolution_convert_fusion
  516.5 5.6 convolution_convert_fusion.6
  522.6 10.1 %collective-permute-done.34 = bf16[320,2048]{1,0:T(8,128)(2,1)S(1)} collective-permute-done((bf16[320,2048]{1,0:T(8,128)(2,1)S(1)}, bf16[320,2048]{1,0:T(8,128)(2,1)S(1)}, u32[]{:S(2)}, u32[]{:S(2)}) %collective-permute-start.34) | collective-permute-done | bytes 1310752 | tf_op jit(solution)/shard_map/ppermute | solution.py:202
  532.7 5.2 fusion.35
  538.0 8.9 convolution_convert_fusion.1
  547.2 4.4 fusion.73
  551.6 71.1 %collective-permute-done.33 = bf16[384,2048]{1,0:T(8,128)(2,1)} collective-permute-done((bf16[384,2048]{1,0:T(8,128)(2,1)}, bf16[384,2048]{1,0:T(8,128)(2,1)}, u32[]{:S(2)}, u32[]{:S(2)}) %collective-permute-start.33) | collective-permute-done | bytes 1572896 | tf_op jit(solution)/shard_map/ppermute | solution.py:202
  622.7 5.9 add_convert_fusion.3
  628.8 9.7 fusion.50
  638.6 15.7 %add_convert_fusion.5 = bf16[384,2048]{1,0:T(8,128)(2,1)} fusion(bf16[1536,640]{0,1:T(8,128)(2,1)} %get-tuple-element.28, bf16[1536,640]{0,1:T(8,128)(2,1)} %copy-done.25, bf16[1536,768]{0,1:T(8,128)(2,1)} %get-tuple-element.26, bf16[1536,768]{0,1:T(8,128)(2,1)} %get-tuple-element.25, bf16[768,2048]{1,0:T(8,128)(2,1)} %collective-permute-done.22, ...), kind=kOutput, calls=%fused_computation.68 | convolution fusion | flops 4486332416 | bytes 23330816 | tf_op jit(solution)/shard_map/dot_general | solution.py:21
  654.6 9.6 add_convert_fusion.1
  664.3 5.6 add_convert_fusion.6
  671.8 20.1 %collective-permute-done.23 = bf16[384,2048]{1,0:T(8,128)(2,1)} collective-permute-done((bf16[384,2048]{1,0:T(8,128)(2,1)}, bf16[384,2048]{1,0:T(8,128)(2,1)}, u32[]{:S(2)}, u32[]{:S(2)}) %collective-permute-start.23) | collective-permute-done | bytes 1572896 | tf_op jit(solution)/shard_map/ppermute | solution.py:202
  697.2 25.8 %collective-permute-done.18 = bf16[384,2048]{1,0:T(8,128)(2,1)S(1)} collective-permute-done((bf16[384,2048]{1,0:T(8,128)(2,1)S(1)}, bf16[384,2048]{1,0:T(8,128)(2,1)S(1)}, u32[]{:S(2)}, u32[]{:S(2)}) %collective-permute-start.18) | collective-permute-done | bytes 1572896 | tf_op jit(solution)/shard_map/ppermute | solution.py:202
  723.0 4.3 fusion.120
  727.6 33.7 %collective-permute-done.24 = bf16[384,2048]{1,0:T(8,128)(2,1)} collective-permute-done((bf16[384,2048]{1,0:T(8,128)(2,1)S(1)}, bf16[384,2048]{1,0:T(8,128)(2,1)}, u32[]{:S(2)}, u32[]{:S(2)}) %collective-permute-start.24) | collective-permute-done | bytes 1572896 | tf_op jit(solution)/shard_map/ppermute | solution.py:202
  761.4 9.1 add_convert_fusion
  773.9 7.8 convolution_convert_fusion.5.refs_0_
  781.7 32.2 %attend_back.1 = bf16[1536,1024]{1,0:T(8,128)(2,1)} custom-call(bf16[1536,512]{1,0:T(8,128)(2,1)} %convolution_convert_fusion.5.refs_0_, bf16[1536,512]{1,0:T(8,128)(2,1)} %get-tuple-element.16.refs_1_, bf16[1536,256]{1,0:T(8,128)(2,1)} %get-tuple-element.17.refs_2_, bf16[1536,256]{1,0:T(8,128)(2,1)} %get-tuple-element.18.refs_3_, ...), custom_call_target="tpu_custom_call" | custom-call | tf_op jit(solution)/shard_map/attend_back/pallas_call | solution.py:172
  814.0 8.0 convolution_convert_fusion.3
  822.6 6.0 convolution_convert_fusion.8
  831.3 3.5 all-to-all-start.5
  834.9 7.8 fusion.58
  844.4 10.6 %collective-permute-done.30 = bf16[256,2048]{1,0:T(8,128)(2,1)} collective-permute-done((bf16[256,2048]{1,0:T(8,128)(2,1)}, bf16[256,2048]{1,0:T(8,128)(2,1)}, u32[]{:S(2)}, u32[]{:S(2)}) %collective-permute-start.30) | collective-permute-done | bytes 1048608 | tf_op jit(solution)/shard_map/ppermute | solution.py:202
  855.0 6.4 fusion.40
  861.5 5.9 fusion.90
  871.8 3.5 all-to-all-start.4
  875.4 6.1 add_convert_fusion.4
  883.4 15.6 %collective-permute-done.29 = bf16[1024,1024]{1,0:T(8,128)(2,1)} collective-permute-done((bf16[1024,1024]{1,0:T(8,128)(2,1)}, bf16[1024,1024]{1,0:T(8,128)(2,1)}, u32[]{:S(2)}, u32[]{:S(2)}) %collective-permute-start.29) | collective-permute-done | bytes 2097184 | tf_op jit(solution)/shard_map/ppermute | solution.py:202
  899.0 7.4 add_convert_fusion.2
  917.7 3.5 reshape.219
  921.2 3.9 fusion.65
  927.4 3.6 convert_add_fusion
  943.4 6.1 reduce-scatter.7.cloned.1.call-done
  949.5 3.5 all-to-all-start.3
  953.0 5.2 fusion.27
  958.2 3.6 all-to-all-done.3
  (363 shorter events, 129.3 us)
Async XLA Ops:
  7.2 78.9 %all-gather.7.cloned.1.call-start = ((), (), s32[]{:S(2)}) async-start(), calls=%async_computation.12 | async-start | bytes 2621440 | tf_op jit(solution)/shard_map/all_gather | solution.py:223
  23.2 146.5 %all-gather.9.cloned.1.call-start = ((), (), s32[]{:S(2)}) async-start(), calls=%async_computation.13 | async-start | bytes 2621440 | tf_op jit(solution)/shard_map/all_gather | solution.py:223
  23.3 8.0 collective-permute-start.7
  26.8 37.9 %copy-start.19 = (bf16[64,5632]{1,0:T(8,128)(2,1)S(1)}, bf16[64,5632]{1,0:T(8,128)(2,1)}, u32[]{:S(2)}) copy-start(bf16[64,5632]{1,0:T(8,128)(2,1)} %param.20) | copy-start | bytes 2162692
  28.9 35.8 %collective-permute-start = (bf16[384,2048]{1,0:T(8,128)(2,1)}, bf16[384,2048]{1,0:T(8,128)(2,1)}, u32[]{:S(2)}, u32[]{:S(2)}) collective-permute-start(bf16[384,2048]{1,0:T(8,128)(2,1)} %pad_maximum_fusion.14), channel_id=1, source_target_pairs={{0,2},{2,0},{1,3},{3,1},{4,6},{6,4},{5,7},{7,5},{8,10},{10,8},{9,1... | collective-permute-start | bytes 4718600 | tf_op jit(solution)/shard_map/ppermute | solution.py:202
  32.2 74.4 %collective-permute-start.1 = (bf16[384,2048]{1,0:T(8,128)(2,1)}, bf16[384,2048]{1,0:T(8,128)(2,1)}, u32[]{:S(2)}, u32[]{:S(2)}) collective-permute-start(bf16[384,2048]{1,0:T(8,128)(2,1)} %pad_maximum_fusion.14), channel_id=1, source_target_pairs={{0,1},{1,0},{2,3},{3,2},{4,5},{5,4},{6,7},{7,6},{8,9},{9,8},{10,11... | collective-permute-start | bytes 4718600 | tf_op jit(solution)/shard_map/ppermute | solution.py:202
  32.3 34.7 %copy-start.64 = (f32[64]{0:T(128)}, f32[64]{0:T(128)S(1)}, u32[]{:S(2)}) copy-start(f32[64]{0:T(128)S(1)} %convert_element_type.274) | copy-start | bytes 772
  64.7 41.9 %collective-permute-start.2 = (bf16[384,2048]{1,0:T(8,128)(2,1)}, bf16[384,2048]{1,0:T(8,128)(2,1)}, u32[]{:S(2)}, u32[]{:S(2)}) collective-permute-start(bf16[384,2048]{1,0:T(8,128)(2,1)} %collective-permute-done), channel_id=1, source_target_pairs={{0,1},{1,0},{2,3},{3,2},{4,5},{5,4},{6,7},{7,6},{8,9},{9,8},{10,11... | collective-permute-start | bytes 4718600 | tf_op jit(solution)/shard_map/ppermute | solution.py:202
  80.6 18.8 %all-to-all-start.1 = ((bf16[4,64,1536]{2,1,0:T(8,128)(2,1)}), bf16[4,64,1536]{2,1,0:T(8,128)(2,1)S(1)}, u32[]{:S(2)}, u32[]{:S(2)}) async-start(bf16[4,64,1536]{2,1,0:T(8,128)(2,1)} %pad_maximum_fusion.22), calls=%async_computation.1 | async-start | bytes 1572864 | tf_op jit(solution)/shard_map/all_to_all | solution.py:231
  84.1 145.3 %all-gather.11.cloned.1.call-start = ((), (), s32[]{:S(2)}) async-start(), calls=%async_computation.14 | async-start | bytes 3932160 | tf_op jit(solution)/shard_map/all_gather | solution.py:223
  84.1 11.6 %collective-permute-start.4 = (s32[2,192]{1,0:T(2,128)S(1)}, s32[2,192]{1,0:T(2,128)S(1)}, u32[]{:S(2)}, u32[]{:S(2)}) collective-permute-start(s32[2,192]{1,0:T(2,128)S(1)} %copy-done.66), channel_id=1, source_target_pairs={{0,2},{2,0},{1,3},{3,1},{4,6},{6,4},{5,7},{7,5},{8,10},{10,8},{9,1... | collective-permute-start | bytes 4616 | tf_op jit(solution)/shard_map/ppermute | solution.py:202
  86.1 9.7 collective-permute-start.5
  86.1 48.4 %collective-permute-start.3 = (bf16[1024,1024]{1,0:T(8,128)(2,1)}, bf16[1024,1024]{1,0:T(8,128)(2,1)}, u32[]{:S(2)}, u32[]{:S(2)}) collective-permute-start(bf16[1024,1024]{1,0:T(8,128)(2,1)} %all-gather.7.cloned.1.call-done), channel_id=1, source_target_pairs={{0,4},{4,0},{1,5},{5,1},{2,6},{6,2},{3,7},{7,3},{8,12},{12,8},{9,1... | collective-permute-start | bytes 6291464 | tf_op jit(solution)/shard_map/ppermute | solution.py:202
  95.7 1.2 collective-permute-start.6
  100.3 138.5 %all-gather.17.cloned.1.call-start = ((), (), s32[]{:S(2)}) async-start(), calls=%async_computation.17 | async-start | bytes 1638400 | tf_op jit(solution)/shard_map/all_gather | solution.py:223
  110.8 25.4 %copy-start.9 = (bf16[1536,2048]{1,0:T(8,128)(2,1)}, bf16[1536,2048]{1,0:T(8,128)(2,1)S(1)}, u32[]{:S(2)}) copy-start(bf16[1536,2048]{1,0:T(8,128)(2,1)S(1)} %pad_maximum_fusion.1) | copy-start | bytes 18874372
  175.2 6.0 collective-permute-start.8
  176.9 74.1 %all-gather.15.cloned.1.call-start = ((), (), s32[]{:S(2)}) async-start(), calls=%async_computation.16 | async-start | bytes 1966080 | tf_op jit(solution)/shard_map/all_gather | solution.py:223
  178.8 182.6 %all-gather.13.cloned.1.call-start = ((), (), s32[]{:S(2)}) async-start(), calls=%async_computation.15 | async-start | bytes 3276800 | tf_op jit(solution)/shard_map/all_gather | solution.py:223
  185.3 47.0 %collective-permute-start.9 = (bf16[384,2048]{1,0:T(8,128)(2,1)}, bf16[384,2048]{1,0:T(8,128)(2,1)}, u32[]{:S(2)}, u32[]{:S(2)}) collective-permute-start(bf16[384,2048]{1,0:T(8,128)(2,1)} %add_convert_fusion.7), channel_id=1, source_target_pairs={{0,2},{2,0},{1,3},{3,1},{4,6},{6,4},{5,7},{7,5},{8,10},{10,8},{9,1... | collective-permute-start | bytes 4718600 | tf_op jit(solution)/shard_map/ppermute | solution.py:202
  229.1 599.8 %reduce-scatter.17.cloned.1.call-start = ((), (), s32[]{:S(2)}) async-start(), calls=%async_computation.23 | async-start | bytes 1638400 | tf_op jit(solution)/shard_map/reduce_scatter | solution.py:227
  229.4 139.1 %collective-permute-start.13 = (bf16[1024,1536]{1,0:T(8,128)(2,1)}, bf16[1024,1536]{1,0:T(8,128)(2,1)}, u32[]{:S(2)}, u32[]{:S(2)}) collective-permute-start(bf16[1024,1536]{1,0:T(8,128)(2,1)} %all-gather.11.cloned.1.call-done), channel_id=1, source_target_pairs={{0,4},{4,0},{1,5},{5,1},{2,6},{6,2},{3,7},{7,3},{8,12},{12,8},{9,1... | collective-permute-start | bytes 9437192 | tf_op jit(solution)/shard_map/ppermute | solution.py:202
  238.5 90.4 %collective-permute-start.10 = (bf16[384,2048]{1,0:T(8,128)(2,1)}, bf16[384,2048]{1,0:T(8,128)(2,1)}, u32[]{:S(2)}, u32[]{:S(2)}) collective-permute-start(bf16[384,2048]{1,0:T(8,128)(2,1)} %pad_maximum_fusion.15), channel_id=1, source_target_pairs={{0,2},{2,0},{1,3},{3,1},{4,6},{6,4},{5,7},{7,5},{8,10},{10,8},{9,1... | collective-permute-start | bytes 4718600 | tf_op jit(solution)/shard_map/ppermute | solution.py:202
  238.8 90.1 %collective-permute-start.16 = (bf16[320,2048]{1,0:T(8,128)(2,1)}, bf16[320,2048]{1,0:T(8,128)(2,1)}, u32[]{:S(2)}, u32[]{:S(2)}) collective-permute-start(bf16[320,2048]{1,0:T(8,128)(2,1)} %all-gather.17.cloned.1.call-done), channel_id=1, source_target_pairs={{0,4},{4,0},{1,5},{5,1},{2,6},{6,2},{3,7},{7,3},{8,12},{12,8},{9,1... | collective-permute-start | bytes 3932168 | tf_op jit(solution)/shard_map/ppermute | solution.py:202
  251.0 110.3 %collective-permute-start.15 = (bf16[384,2048]{1,0:T(8,128)(2,1)}, bf16[384,2048]{1,0:T(8,128)(2,1)}, u32[]{:S(2)}, u32[]{:S(2)}) collective-permute-start(bf16[384,2048]{1,0:T(8,128)(2,1)} %all-gather.15.cloned.1.call-done), channel_id=1, source_target_pairs={{0,4},{4,0},{1,5},{5,1},{2,6},{6,2},{3,7},{7,3},{8,12},{12,8},{9,1... | collective-permute-start | bytes 4718600 | tf_op jit(solution)/shard_map/ppermute | solution.py:202
  252.7 112.5 %copy-start.60 = (f32[384]{0:T(512)}, f32[384]{0:T(512)S(1)}, u32[]{:S(2)}) copy-start(f32[384]{0:T(512)S(1)} %reshape.221) | copy-start | bytes 4612
  254.2 114.4 %collective-permute-start.19 = (bf16[384,2048]{1,0:T(8,128)(2,1)}, bf16[384,2048]{1,0:T(8,128)(2,1)}, u32[]{:S(2)}, u32[]{:S(2)}) collective-permute-start(bf16[384,2048]{1,0:T(8,128)(2,1)} %fusion.22), channel_id=1, source_target_pairs={{0,2},{2,0},{1,3},{3,1},{4,6},{6,4},{5,7},{7,5},{8,10},{10,8},{9,1... | collective-permute-start | bytes 4718600 | tf_op jit(solution)/shard_map/ppermute | solution.py:202
  328.8 40.2 %collective-permute-start.11 = (bf16[384,2048]{1,0:T(8,128)(2,1)}, bf16[384,2048]{1,0:T(8,128)(2,1)S(1)}, u32[]{:S(2)}, u32[]{:S(2)}) collective-permute-start(bf16[384,2048]{1,0:T(8,128)(2,1)} %pad_maximum_fusion.15), channel_id=1, source_target_pairs={{0,1},{1,0},{2,3},{3,2},{4,5},{5,4},{6,7},{7,6},{8,9},{9,8},{10,11... | collective-permute-start | bytes 4718600 | tf_op jit(solution)/shard_map/ppermute | solution.py:202
  328.8 40.2 %collective-permute-start.12 = (bf16[384,2048]{1,0:T(8,128)(2,1)}, bf16[384,2048]{1,0:T(8,128)(2,1)}, u32[]{:S(2)}, u32[]{:S(2)}) collective-permute-start(bf16[384,2048]{1,0:T(8,128)(2,1)} %collective-permute-done.10), channel_id=1, source_target_pairs={{0,1},{1,0},{2,3},{3,2},{4,5},{5,4},{6,7},{7,6},{8,9},{9,8},{10,11... | collective-permute-start | bytes 4718600 | tf_op jit(solution)/shard_map/ppermute | solution.py:202
  361.3 58.0 %collective-permute-start.14 = (bf16[1024,1280]{1,0:T(8,128)(2,1)}, bf16[1024,1280]{1,0:T(8,128)(2,1)}, u32[]{:S(2)}, u32[]{:S(2)}) collective-permute-start(bf16[1024,1280]{1,0:T(8,128)(2,1)} %all-gather.13.cloned.1.call-done), channel_id=1, source_target_pairs={{0,4},{4,0},{1,5},{5,1},{2,6},{6,2},{3,7},{7,3},{8,12},{12,8},{9,1... | collective-permute-start | bytes 7864328 | tf_op jit(solution)/shard_map/ppermute | solution.py:202
  368.5 65.8 %collective-permute-start.20 = (bf16[384,2048]{1,0:T(8,128)(2,1)}, bf16[384,2048]{1,0:T(8,128)(2,1)}, u32[]{:S(2)}, u32[]{:S(2)}) collective-permute-start(bf16[384,2048]{1,0:T(8,128)(2,1)} %fusion.22), channel_id=1, source_target_pairs={{0,1},{1,0},{2,3},{3,2},{4,5},{5,4},{6,7},{7,6},{8,9},{9,8},{10,11... | collective-permute-start | bytes 4718600 | tf_op jit(solution)/shard_map/ppermute | solution.py:202
  368.5 65.7 %collective-permute-start.21 = (bf16[384,2048]{1,0:T(8,128)(2,1)}, bf16[384,2048]{1,0:T(8,128)(2,1)}, u32[]{:S(2)}, u32[]{:S(2)}) collective-permute-start(bf16[384,2048]{1,0:T(8,128)(2,1)} %collective-permute-done.19), channel_id=1, source_target_pairs={{0,1},{1,0},{2,3},{3,2},{4,5},{5,4},{6,7},{7,6},{8,9},{9,8},{10,11... | collective-permute-start | bytes 4718600 | tf_op jit(solution)/shard_map/ppermute | solution.py:202
  369.0 50.3 %copy-start.27 = (bf16[384,2048]{1,0:T(8,128)(2,1)}, bf16[384,2048]{1,0:T(8,128)(2,1)S(1)}, u32[]{:S(2)}) copy-start(bf16[384,2048]{1,0:T(8,128)(2,1)S(1)} %collective-permute-done.11) | copy-start | bytes 4718596
  447.2 61.6 %copy-start.25 = (bf16[1536,640]{0,1:T(8,128)(2,1)}, bf16[1536,640]{0,1:T(8,128)(2,1)S(1)}, u32[]{:S(2)}) copy-start(bf16[1536,640]{0,1:T(8,128)(2,1)S(1)} %get-tuple-element.27) | copy-start | bytes 5898244
  487.0 151.5 %collective-permute-start.22 = (bf16[768,2048]{1,0:T(8,128)(2,1)}, bf16[768,2048]{1,0:T(8,128)(2,1)}, u32[]{:S(2)}, u32[]{:S(2)}) collective-permute-start(bf16[768,2048]{1,0:T(8,128)(2,1)} %fusion.10), channel_id=1, source_target_pairs={{0,1},{1,0},{2,3},{3,2},{4,5},{5,4},{6,7},{7,6},{8,9},{9,8},{10,11... | collective-permute-start | bytes 9437192 | tf_op jit(solution)/shard_map/ppermute | solution.py:202
  496.1 168.2 %collective-permute-start.17 = (bf16[768,2048]{1,0:T(8,128)(2,1)}, bf16[768,2048]{1,0:T(8,128)(2,1)}, u32[]{:S(2)}, u32[]{:S(2)}) collective-permute-start(bf16[768,2048]{1,0:T(8,128)(2,1)} %convolution_convert_fusion.4), channel_id=1, source_target_pairs={{0,1},{1,0},{2,3},{3,2},{4,5},{5,4},{6,7},{7,6},{8,9},{9,8},{10,11... | collective-permute-start | bytes 9437192 | tf_op jit(solution)/shard_map/ppermute | solution.py:202
  501.0 31.7 %collective-permute-start.34 = (bf16[320,2048]{1,0:T(8,128)(2,1)S(1)}, bf16[320,2048]{1,0:T(8,128)(2,1)S(1)}, u32[]{:S(2)}, u32[]{:S(2)}) collective-permute-start(bf16[320,2048]{1,0:T(8,128)(2,1)S(1)} %convolution_convert_fusion.7), channel_id=1, source_target_pairs={{0,4},{4,0},{1,5},{5,1},{2,6},{6,2},{3,7},{7,3},{8,12},{12,8},{9,1... | collective-permute-start | bytes 3932168 | tf_op jit(solution)/shard_map/ppermute | solution.py:202
  515.0 139.7 %collective-permute-start.32 = (bf16[1024,1280]{1,0:T(8,128)(2,1)}, bf16[1024,1280]{1,0:T(8,128)(2,1)}, u32[]{:S(2)}, u32[]{:S(2)}) collective-permute-start(bf16[1024,1280]{1,0:T(8,128)(2,1)} %convolution_convert_fusion), channel_id=1, source_target_pairs={{0,4},{4,0},{1,5},{5,1},{2,6},{6,2},{3,7},{7,3},{8,12},{12,8},{9,1... | collective-permute-start | bytes 7864328 | tf_op jit(solution)/shard_map/ppermute | solution.py:202
  522.2 100.5 %collective-permute-start.33 = (bf16[384,2048]{1,0:T(8,128)(2,1)}, bf16[384,2048]{1,0:T(8,128)(2,1)}, u32[]{:S(2)}, u32[]{:S(2)}) collective-permute-start(bf16[384,2048]{1,0:T(8,128)(2,1)} %convolution_convert_fusion.6), channel_id=1, source_target_pairs={{0,4},{4,0},{1,5},{5,1},{2,6},{6,2},{3,7},{7,3},{8,12},{12,8},{9,1... | collective-permute-start | bytes 4718600 | tf_op jit(solution)/shard_map/ppermute | solution.py:202
  537.9 291.0 %reduce-scatter.15.cloned.1.call-start = ((), (), s32[]{:S(2)}) async-start(), calls=%async_computation.22 | async-start | bytes 1966080 | tf_op jit(solution)/shard_map/reduce_scatter | solution.py:227
  546.9 214.4 %collective-permute-start.31 = (bf16[1024,1536]{1,0:T(8,128)(2,1)}, bf16[1024,1536]{1,0:T(8,128)(2,1)}, u32[]{:S(2)}, u32[]{:S(2)}) collective-permute-start(bf16[1024,1536]{1,0:T(8,128)(2,1)} %convolution_convert_fusion.1), channel_id=1, source_target_pairs={{0,4},{4,0},{1,5},{5,1},{2,6},{6,2},{3,7},{7,3},{8,12},{12,8},{9,1... | collective-permute-start | bytes 9437192 | tf_op jit(solution)/shard_map/ppermute | solution.py:202
  628.6 202.7 %reduce-scatter.13.cloned.1.call-start = ((), (), s32[]{:S(2)}) async-start(), calls=%async_computation.21 | async-start | bytes 3276800 | tf_op jit(solution)/shard_map/reduce_scatter | solution.py:227
  654.3 37.6 %collective-permute-start.23 = (bf16[384,2048]{1,0:T(8,128)(2,1)}, bf16[384,2048]{1,0:T(8,128)(2,1)}, u32[]{:S(2)}, u32[]{:S(2)}) collective-permute-start(bf16[384,2048]{1,0:T(8,128)(2,1)} %add_convert_fusion.5), channel_id=1, source_target_pairs={{0,2},{2,0},{1,3},{3,1},{4,6},{6,4},{5,7},{7,5},{8,10},{10,8},{9,1... | collective-permute-start | bytes 4718600 | tf_op jit(solution)/shard_map/ppermute | solution.py:202
  664.3 207.5 %reduce-scatter.11.cloned.1.call-start = ((), (), s32[]{:S(2)}) async-start(), calls=%async_computation.20 | async-start | bytes 3932160 | tf_op jit(solution)/shard_map/reduce_scatter | solution.py:227
  670.0 53.0 %collective-permute-start.18 = (bf16[384,2048]{1,0:T(8,128)(2,1)S(1)}, bf16[384,2048]{1,0:T(8,128)(2,1)S(1)}, u32[]{:S(2)}, u32[]{:S(2)}) collective-permute-start(bf16[384,2048]{1,0:T(8,128)(2,1)S(1)} %add_convert_fusion.6), channel_id=1, source_target_pairs={{0,2},{2,0},{1,3},{3,1},{4,6},{6,4},{5,7},{7,5},{8,10},{10,8},{9,1... | collective-permute-start | bytes 4718600 | tf_op jit(solution)/shard_map/ppermute | solution.py:202
  696.7 26.3 %copy-start.12 = (bf16[2,192,2048]{2,1,0:T(8,128)(2,1)S(1)}, bf16[2,192,2048]{2,1,0:T(8,128)(2,1)}, u32[]{:S(2)}) copy-start(bf16[2,192,2048]{2,1,0:T(8,128)(2,1)} %param.25) | copy-start | bytes 4718596
  696.7 26.3 %copy-start.18 = (f32[384,2048]{1,0:T(8,128)S(1)}, f32[384,2048]{1,0:T(8,128)}, u32[]{:S(2)}) copy-start(f32[384,2048]{1,0:T(8,128)} %fusion.73) | copy-start | bytes 9437188
  696.7 26.3 %copy-start.61 = (f32[384]{0:T(512)S(1)}, f32[384]{0:T(512)}, u32[]{:S(2)}) copy-start(f32[384]{0:T(512)} %copy-done.60) | copy-start | bytes 4612
  697.1 64.2 %slice-start = ((s8[6291456]{0:T(1024)(128)(4,1)}), s8[4194304]{0:T(1024)(128)(4,1)S(1)}, s32[]{:S(2)}) async-start(s8[6291456]{0:T(1024)(128)(4,1)} %bitcast.81), calls=%async_computation.24 | async-start | bytes 8388608
  697.1 64.2 %slice-start.1 = ((s8[6291456]{0:T(1024)(128)(4,1)}), s8[2097152]{0:T(1024)(128)(4,1)S(1)}, s32[]{:S(2)}) async-start(s8[6291456]{0:T(1024)(128)(4,1)} %bitcast.81), calls=%async_computation.25 | async-start | bytes 4194304
  697.1 64.2 %copy-start.21 = (bf16[1536,768]{0,1:T(8,128)(2,1)S(1)}, bf16[1536,768]{0,1:T(8,128)(2,1)}, u32[]{:S(2)}) copy-start(bf16[1536,768]{0,1:T(8,128)(2,1)} %get-tuple-element.25) | copy-start | bytes 7077892
  697.2 64.2 %copy-start.22 = (bf16[1536,768]{0,1:T(8,128)(2,1)S(1)}, bf16[1536,768]{0,1:T(8,128)(2,1)}, u32[]{:S(2)}) copy-start(bf16[1536,768]{0,1:T(8,128)(2,1)} %get-tuple-element.26) | copy-start | bytes 7077892
  727.3 34.0 %collective-permute-start.24 = (bf16[384,2048]{1,0:T(8,128)(2,1)S(1)}, bf16[384,2048]{1,0:T(8,128)(2,1)}, u32[]{:S(2)}, u32[]{:S(2)}) collective-permute-start(bf16[384,2048]{1,0:T(8,128)(2,1)S(1)} %get-tuple-element.21), channel_id=1, source_target_pairs={{0,2},{2,0},{1,3},{3,1},{4,6},{6,4},{5,7},{7,5},{8,10},{10,8},{9,1... | collective-permute-start | bytes 4718600 | tf_op jit(solution)/shard_map/ppermute | solution.py:202
  727.6 46.3 %collective-permute-start.25 = (bf16[384,2048]{1,0:T(8,128)(2,1)S(1)}, bf16[384,2048]{1,0:T(8,128)(2,1)}, u32[]{:S(2)}, u32[]{:S(2)}) collective-permute-start(bf16[384,2048]{1,0:T(8,128)(2,1)S(1)} %get-tuple-element.21), channel_id=1, source_target_pairs={{0,1},{1,0},{2,3},{3,2},{4,5},{5,4},{6,7},{7,6},{8,9},{9,8},{10,11... | collective-permute-start | bytes 4718600 | tf_op jit(solution)/shard_map/ppermute | solution.py:202
  761.3 12.6 %collective-permute-start.26 = (bf16[384,2048]{1,0:T(8,128)(2,1)}, bf16[384,2048]{1,0:T(8,128)(2,1)}, u32[]{:S(2)}, u32[]{:S(2)}) collective-permute-start(bf16[384,2048]{1,0:T(8,128)(2,1)} %collective-permute-done.24), channel_id=1, source_target_pairs={{0,1},{1,0},{2,3},{3,2},{4,5},{5,4},{6,7},{7,6},{8,9},{9,8},{10,11... | collective-permute-start | bytes 4718600 | tf_op jit(solution)/shard_map/ppermute | solution.py:202
  822.0 53.3 %collective-permute-start.27 = (bf16[768,2048]{1,0:T(8,128)(2,1)}, bf16[768,2048]{1,0:T(8,128)(2,1)}, u32[]{:S(2)}, u32[]{:S(2)}) collective-permute-start(bf16[768,2048]{1,0:T(8,128)(2,1)} %convolution_convert_fusion.3), channel_id=1, source_target_pairs={{0,1},{1,0},{2,3},{3,2},{4,5},{5,4},{6,7},{7,6},{8,9},{9,8},{10,11... | collective-permute-start | bytes 9437192 | tf_op jit(solution)/shard_map/ppermute | solution.py:202
  828.6 26.3 %collective-permute-start.30 = (bf16[256,2048]{1,0:T(8,128)(2,1)}, bf16[256,2048]{1,0:T(8,128)(2,1)}, u32[]{:S(2)}, u32[]{:S(2)}) collective-permute-start(bf16[256,2048]{1,0:T(8,128)(2,1)} %convolution_convert_fusion.8), channel_id=1, source_target_pairs={{0,4},{4,0},{1,5},{5,1},{2,6},{6,2},{3,7},{7,3},{8,12},{12,8},{9,1... | collective-permute-start | bytes 3145736 | tf_op jit(solution)/shard_map/ppermute | solution.py:202
  831.3 36.1 %all-to-all-start.5 = ((bf16[4,64,1280]{2,1,0:T(8,128)(2,1)}), bf16[4,64,1280]{2,1,0:T(8,128)(2,1)S(1)}, u32[]{:S(2)}, u32[]{:S(2)}) async-start(bf16[4,64,1280]{2,1,0:T(8,128)(2,1)} %bitcast.107), calls=%async_computation.9 | async-start | bytes 1310720 | tf_op jit(solution)/shard_map/all_to_all | solution.py:231
  834.8 90.9 %reduce-scatter.9.cloned.1.call-start = ((), (), s32[]{:S(2)}) async-start(), calls=%async_computation.19 | async-start | bytes 1310720 | tf_op jit(solution)/shard_map/reduce_scatter | solution.py:227
  842.6 56.3 %collective-permute-start.29 = (bf16[1024,1024]{1,0:T(8,128)(2,1)}, bf16[1024,1024]{1,0:T(8,128)(2,1)}, u32[]{:S(2)}, u32[]{:S(2)}) collective-permute-start(bf16[1024,1024]{1,0:T(8,128)(2,1)} %fusion.58), channel_id=1, source_target_pairs={{0,4},{4,0},{1,5},{5,1},{2,6},{6,2},{3,7},{7,3},{8,12},{12,8},{9,1... | collective-permute-start | bytes 6291464 | tf_op jit(solution)/shard_map/ppermute | solution.py:202
  871.8 34.5 %all-to-all-start.4 = ((bf16[4,64,1536]{2,1,0:T(8,128)(2,1)}), bf16[4,64,1536]{2,1,0:T(8,128)(2,1)S(1)}, u32[]{:S(2)}, u32[]{:S(2)}) async-start(bf16[4,64,1536]{2,1,0:T(8,128)(2,1)} %bitcast.106), calls=%async_computation.7 | async-start | bytes 1572864 | tf_op jit(solution)/shard_map/all_to_all | solution.py:231
  875.3 74.2 %reduce-scatter.7.cloned.1.call-start = ((), (), s32[]{:S(2)}) async-start(), calls=%async_computation.18 | async-start | bytes 2621440 | tf_op jit(solution)/shard_map/reduce_scatter | solution.py:227
  881.5 46.0 %collective-permute-start.28 = (bf16[384,2048]{1,0:T(8,128)(2,1)}, bf16[384,2048]{1,0:T(8,128)(2,1)}, u32[]{:S(2)}, u32[]{:S(2)}) collective-permute-start(bf16[384,2048]{1,0:T(8,128)(2,1)} %add_convert_fusion.4), channel_id=1, source_target_pairs={{0,2},{2,0},{1,3},{3,1},{4,6},{6,4},{5,7},{7,5},{8,10},{10,8},{9,1... | collective-permute-start | bytes 4718600 | tf_op jit(solution)/shard_map/ppermute | solution.py:202
  949.5 12.3 %all-to-all-start.3 = ((bf16[4,64,1024]{2,1,0:T(8,128)(2,1)}), bf16[4,64,1024]{2,1,0:T(8,128)(2,1)S(1)}, u32[]{:S(2)}, u32[]{:S(2)}) async-start(bf16[4,64,1024]{2,1,0:T(8,128)(2,1)} %bitcast.108), calls=%async_computation.4 | async-start | bytes 1048576 | tf_op jit(solution)/shard_map/all_to_all | solution.py:231
  (63 other events, 507.4 us)
Sparse Core Ops, SparseCore 0:
  23.3 46.3 all-gather.6
  71.9 44.4 all-gather.8
  118.0 62.2 all-gather.10
  181.7 31.1 all-gather.16
  214.9 36.1 all-gather.14
  252.5 53.5 all-gather.12
  538.0 30.7 reduce-scatter.16
  628.7 34.7 reduce-scatter.14
  665.9 51.3 reduce-scatter.12
  770.6 59.8 reduce-scatter.10
  861.6 26.6 reduce-scatter.8
  906.5 43.0 reduce-scatter.6
